TPU v7x, 32 devices: a whole 2x2x4 slice. The times are simulated.
32 devices in a mesh: dp: 8 (over z, y), col: 4 (over x, core).
Axes of the slice: x: 2, y: 2, z: 4, core: 2. Of those that a mesh axis runs over, the one named last changes fastest.
Arguments:
- tokens: bfloat16 [8192, 8192], P('dp', 'col'), may hold values from -6 to 6
- out_grad: bfloat16 [8192, 8192], P(('dp', 'col')), may hold values from -6 to 6
- weight: float32 [8192, 8192], P('dp', 'col'), may hold values from -6 to 6
- second: float32 [8192, 8192], P('dp', 'col'), may hold values from 0.0001 to 0.001
- momentum: float32 [8192, 512], P(('dp', 'col')), may hold values from -0.12 to 0.12
- sign_seed: int32 [1], replicated, may hold values from 0 to 999999
- step_number: int32 [1], replicated, may hold values from 1 to 999999
Outputs:
- new_weight: float32 [8192, 8192], P('dp', 'col')
- new_second: float32 [8192, 8192], P('dp', 'col')
- new_momentum: float32 [8192, 512], P(('dp', 'col'))
All inputs are finite; a program needn't handle non-finite values.
Results may differ from a plain program's by a relative error of at most 0.00097.
Values may be sent and summed in bfloat16 or wider, within the bound.
No kernel may reach another device: no remote copies, remote signals or barrier semaphores. Data moves between devices by JAX's collectives and lax.ppermute only.
A program may use at most 128 MiB of HBM per device.

v0:
```python
import functools

import jax
import jax.numpy as jnp
from jax import lax
from jax.experimental import pallas as pl
from jax.experimental.pallas import tpu as pltpu
from jax.sharding import PartitionSpec as P


AXES = ("dp", "col")
LANES = 128


def hashed_signs(flat_scaled, sign_seed, step_number):
    hashed = flat_scaled + sign_seed * 1664525 + step_number * 1013904223
    hashed = hashed ^ hashed >> 16 & 65535
    hashed = hashed * 2127912213
    hashed = hashed ^ hashed >> 13 & 524287
    hashed = hashed * 1103515245
    hashed = hashed ^ hashed >> 16 & 65535
    return hashed >> 20 & 1


def sign_table(sign_seed, step_number, first_row, row_count, low_rank):
    row_ids = first_row + lax.iota(jnp.int32, row_count)
    col_ids = lax.iota(jnp.int32, low_rank)
    flat_index = row_ids[:, None] * low_rank + col_ids[None, :]
    low_bit = hashed_signs(flat_index * 747796405, sign_seed[0], step_number[0])
    return (1 - 2 * low_bit).astype(jnp.float32)


def contract(left_rows, right_rows):
    return lax.dot_general(
        left_rows, right_rows, (((0,), (0,)), ((), ())), preferred_element_type=jnp.float32
    )


def general(tokens, out_grad, weight, second, momentum, sign_seed, step_number):
    local_tokens, din_local = tokens.shape
    low_rank = momentum.shape[1]
    owner_rows = momentum.shape[0]
    inv_root = 1.0 / jnp.sqrt(jnp.float32(low_rank))
    col_position = lax.axis_index("col")
    sign_block = sign_table(sign_seed, step_number, col_position * din_local, din_local, low_rank)
    partial_sketch = (
        jnp.dot(tokens, sign_block.astype(jnp.bfloat16), preferred_element_type=jnp.float32)
        * inv_root
    )
    quarter = lax.psum_scatter(partial_sketch, "col", scatter_dimension=0, tiled=True)
    sketch = quarter.astype(jnp.bfloat16)
    total_tokens = lax.axis_size("dp") * local_tokens
    data_count = lax.axis_size("dp")
    col_count = lax.axis_size("col")
    quarter_rows = out_grad.shape[0]
    grouped = out_grad.reshape(quarter_rows, data_count, col_count, owner_rows)
    grouped = jnp.transpose(grouped, (0, 2, 1, 3)).reshape(
        quarter_rows, col_count, data_count * owner_rows
    )
    regrouped = lax.all_to_all(grouped, "col", split_axis=1, concat_axis=0, tiled=True)
    regrouped = regrouped.reshape(quarter_rows * col_count, data_count * owner_rows)
    shard_sketch = lax.all_gather(sketch, "col", axis=0, tiled=True)
    projected = lax.psum_scatter(
        contract(regrouped, shard_sketch), "dp", scatter_dimension=0, tiled=True
    )
    projected = projected / jnp.float32(total_tokens)
    new_momentum = 0.8 * momentum + 0.2 * projected
    row_block = lax.all_gather(new_momentum, "col", axis=0, tiled=True)
    dense_grad = (
        lax.dot_general(
            row_block,
            sign_block,
            (((1,), (1,)), ((), ())),
            precision=lax.Precision.HIGHEST,
            preferred_element_type=jnp.float32,
        )
        * inv_root
    )
    new_second = 0.95 * second + 0.05 * dense_grad * dense_grad
    new_weight = weight - 0.5 * dense_grad / (jnp.sqrt(new_second) + 1e-08)
    return (new_weight, new_second, new_momentum)


def params(vmem=56 * 1024 * 1024, axes=1):
    return pltpu.CompilerParams(
        dimension_semantics=("arbitrary",) * axes, vmem_limit_bytes=vmem
    )


def pack_kernel(groups, width, part, og_ref, *refs):
    n_out = len(groups)
    outs = refs[:n_out]
    stage, in_sem, out_sem = refs[n_out:]
    me = lax.axis_index("dp") * lax.axis_size("col") + lax.axis_index("col")
    loads = []
    slot = 0
    for group in groups:
        mine = []
        for rel, half in group:
            first = pl.multiple_of((me ^ rel) * width + half * part, part)
            copy = pltpu.make_async_copy(
                og_ref.at[:, pl.ds(first, part)], stage.at[slot], in_sem.at[slot]
            )
            copy.start()
            mine.append(copy)
            slot += 1
        loads.append(mine)
    stores = []
    slot = 0
    for index, group in enumerate(groups):
        for copy in loads[index]:
            copy.wait()
        store = pltpu.make_async_copy(
            stage.at[pl.ds(slot, len(group))], outs[index], out_sem.at[index]
        )
        store.start()
        stores.append(store)
        slot += len(group)
    for store in stores:
        store.wait()


def pack(out_grad, groups, width, part):
    rows = out_grad.shape[0]
    count = sum(len(group) for group in groups)
    return pl.pallas_call(
        functools.partial(pack_kernel, groups, width, part),
        in_specs=[pl.BlockSpec(memory_space=pl.ANY)],
        out_specs=[pl.BlockSpec(memory_space=pl.ANY)] * len(groups),
        out_shape=[
            jax.ShapeDtypeStruct((len(group), rows, part), out_grad.dtype) for group in groups
        ],
        scratch_shapes=[
            pltpu.VMEM((count, rows, part), out_grad.dtype),
            pltpu.SemaphoreType.DMA((count,)),
            pltpu.SemaphoreType.DMA((len(groups),)),
        ],
        compiler_params=pltpu.CompilerParams(vmem_limit_bytes=16 * 1024 * 1024),
        cost_estimate=pl.CostEstimate(
            flops=0, bytes_accessed=4 * count * rows * part, transcendentals=0
        ),
        name="pack",
    )(pltpu.with_memory_space_constraint(out_grad, pltpu.HBM))


def split_acc(place_ref, acc, send_ref, keep_ref):
    rows = keep_ref.shape[0]
    core = place_ref[0] & 1
    keep_ref[...] = acc[pl.ds(pl.multiple_of(core * rows, rows), rows), :]
    send_ref[...] = acc[pl.ds(pl.multiple_of((1 - core) * rows, rows), rows), :]


def sketch_first(steps, chunk, din_local, place_ref, tok_ref, signs_ref, send_ref, keep_ref, acc):
    step = pl.program_id(0)
    low_rank = signs_ref.shape[1]
    shape = (chunk, low_rank)
    first = place_ref[0] * din_local + step * chunk
    flat = (first + lax.broadcasted_iota(jnp.int32, shape, 0)) * low_rank
    flat = flat + lax.broadcasted_iota(jnp.int32, shape, 1)
    low_bit = hashed_signs(flat * 747796405, place_ref[1], place_ref[2])
    signs = jnp.where(low_bit == 1, -1.0, 1.0).astype(jnp.bfloat16)
    signs_ref[...] = signs
    part = jnp.dot(tok_ref[...], signs, preferred_element_type=jnp.float32)

    @pl.when(step == 0)
    def _():
        acc[...] = part

    @pl.when(step > 0)
    def _():
        acc[...] += part

    @pl.when(step == steps - 1)
    def _():
        split_acc(place_ref, acc, send_ref, keep_ref)


def sketch_next(steps, place_ref, tok_ref, signs_ref, send_ref, keep_ref, acc):
    step = pl.program_id(0)
    part = jnp.dot(tok_ref[...], signs_ref[...], preferred_element_type=jnp.float32)

    @pl.when(step == 0)
    def _():
        acc[...] = part

    @pl.when(step > 0)
    def _():
        acc[...] += part

    @pl.when(step == steps - 1)
    def _():
        split_acc(place_ref, acc, send_ref, keep_ref)


def sketch_parts(place, tokens, low_rank, signs):
    local_tokens, din_local = tokens.shape
    chunk = din_local // 4
    steps = din_local // chunk
    half = local_tokens // 2
    quarter = half // 2
    first = signs is None
    tok_spec = pl.BlockSpec(
        (half, chunk), lambda i, p: ((p[0] >> 1) ^ (1 if first else 0), i)
    )
    sign_spec = pl.BlockSpec((chunk, low_rank), lambda i, p: (i, 0))
    part_spec = pl.BlockSpec((quarter, low_rank), lambda i, p: (0, 0))
    parts = [jax.ShapeDtypeStruct((quarter, low_rank), jnp.float32)] * 2
    if first:
        body = functools.partial(sketch_first, steps, chunk, din_local)
        in_specs, args = [tok_spec], (tokens,)
        out_specs = [sign_spec, part_spec, part_spec]
        out_shape = [jax.ShapeDtypeStruct((din_local, low_rank), jnp.bfloat16)] + parts
    else:
        body = functools.partial(sketch_next, steps)
        in_specs, args = [tok_spec, sign_spec], (tokens, signs)
        out_specs = [part_spec, part_spec]
        out_shape = parts
    return pl.pallas_call(
        body,
        grid_spec=pltpu.PrefetchScalarGridSpec(
            num_scalar_prefetch=1,
            grid=(steps,),
            in_specs=in_specs,
            out_specs=out_specs,
            scratch_shapes=[pltpu.VMEM((half, low_rank), jnp.float32)],
        ),
        out_shape=out_shape,
        compiler_params=params(24 * 1024 * 1024),
        cost_estimate=pl.CostEstimate(
            flops=2 * half * din_local * low_rank,
            bytes_accessed=half * din_local * 2 + din_local * low_rank * 2 + 2 * half * low_rank * 4,
            transcendentals=0,
        ),
        name="sketch_first" if first else "sketch_next",
    )(place, *args)


def project_kernel(n, *refs):
    send_ref, keep_ref = refs[-2:]
    count, _, part = refs[n].shape
    sketch = jnp.concatenate([ref[...] for ref in refs[:n]], axis=0)
    grads = jnp.concatenate(
        [
            jnp.concatenate([ref[j] for j in range(count)], axis=1)
            for ref in refs[n : 2 * n]
        ],
        axis=0,
    )
    total = contract(grads, sketch)
    for j in range(count):
        out_ref = send_ref if j < count // 2 else keep_ref
        out_ref[j % (count // 2)] = total[j * part : (j + 1) * part]


def project(sketches, grads, offsets, count):
    rows, low_rank = sketches[0].shape
    part = grads[0].shape[2]
    n = len(sketches)

    def block_at(offset):
        return pl.BlockSpec((count, rows, part), lambda i: (offset // count, 0, 0))

    out = jax.ShapeDtypeStruct((count // 2, part, low_rank), jnp.float32)
    return pl.pallas_call(
        functools.partial(project_kernel, n),
        grid=(1,),
        in_specs=[pl.BlockSpec((rows, low_rank), lambda i: (0, 0))] * n
        + [block_at(offset) for offset in offsets],
        out_specs=[pl.BlockSpec((count // 2, part, low_rank), lambda i: (0, 0, 0))] * 2,
        out_shape=[out] * 2,
        compiler_params=params(16 * 1024 * 1024),
        cost_estimate=pl.CostEstimate(
            flops=2 * n * count * rows * part * low_rank,
            bytes_accessed=n * (rows * low_rank + count * rows * part) * 2
            + count * low_rank * part * 4,
            transcendentals=0,
        ),
        name="project",
    )(*sketches, *grads)


def update_kernel(relatives, half, place_ref, *refs):
    n = len(relatives)
    rows_refs = refs[:n]
    signs_ref, weight_ref, second_ref = refs[n : n + 3]
    new_weight_ref, new_second_ref, w_buf, s_buf, nw_buf, ns_buf, in_sem, out_sem = refs[-8:]
    part, low_rank = rows_refs[0].shape
    width = signs_ref.shape[0]
    chunk = width // 2
    inv_root = 1.0 / jnp.sqrt(jnp.full((1, 1), low_rank, jnp.float32))
    nt = (((1,), (1,)), ((), ()))
    tasks = []
    for index, rel in enumerate(relatives):
        first = pl.multiple_of(((place_ref[0] ^ rel) * 2 + half) * part, part)
        for at in range(0, width, chunk):
            slot = len(tasks)
            window = (pl.ds(first, part), pl.ds(at, chunk))
            loads = [
                pltpu.make_async_copy(weight_ref.at[window], w_buf.at[slot], in_sem.at[0, slot]),
                pltpu.make_async_copy(second_ref.at[window], s_buf.at[slot], in_sem.at[1, slot]),
            ]
            for load in loads:
                load.start()
            tasks.append((index, at, window, loads))
    stores = []
    for slot, (index, at, window, loads) in enumerate(tasks):
        rows = rows_refs[index][...]
        high = rows.astype(jnp.bfloat16)
        low = (rows - high.astype(jnp.float32)).astype(jnp.bfloat16)
        signs = signs_ref[at : at + chunk, :]
        dense_grad = lax.dot_general(high, signs, nt, preferred_element_type=jnp.float32)
        dense_grad += lax.dot_general(low, signs, nt, preferred_element_type=jnp.float32)
        dense_grad = dense_grad * inv_root
        for load in loads:
            load.wait()
        new_second = 0.95 * s_buf[slot] + 0.05 * dense_grad * dense_grad
        ns_buf[slot] = new_second
        nw_buf[slot] = w_buf[slot] - 0.5 * dense_grad / (jnp.sqrt(new_second) + 1e-08)
        for kind, (buf, ref) in enumerate(((nw_buf, new_weight_ref), (ns_buf, new_second_ref))):
            store = pltpu.make_async_copy(buf.at[slot], ref.at[window], out_sem.at[kind, slot])
            store.start()
            stores.append(store)
    for store in stores:
        store.wait()


def update(place, row_blocks, relatives, half, signs, weight, second, onto):
    part, low_rank = row_blocks[0].shape
    din_local = weight.shape[1]
    n = len(row_blocks)
    slots, chunk = 2 * n, din_local // 2
    hbm = pl.BlockSpec(memory_space=pl.ANY)
    vmem = pl.BlockSpec(memory_space=pltpu.VMEM)
    in_specs = [pl.BlockSpec(memory_space=pltpu.SMEM)] + [vmem] * (n + 1) + [hbm, hbm]
    aliases = {}
    if onto:
        in_specs += [hbm, hbm]
        aliases = {n + 4: 0, n + 5: 1}
    size = n * part * din_local
    buf = pltpu.VMEM((slots, part, chunk), jnp.float32)
    return pl.pallas_call(
        functools.partial(update_kernel, relatives, half),
        in_specs=in_specs,
        out_specs=[hbm, hbm],
        out_shape=[
            jax.ShapeDtypeStruct(weight.shape, jnp.float32),
            jax.ShapeDtypeStruct(second.shape, jnp.float32),
        ],
        scratch_shapes=[buf] * 4
        + [pltpu.SemaphoreType.DMA((2, slots)), pltpu.SemaphoreType.DMA((2, slots))],
        input_output_aliases=aliases,
        compiler_params=pltpu.CompilerParams(vmem_limit_bytes=24 * 1024 * 1024),
        cost_estimate=pl.CostEstimate(
            flops=4 * size * low_rank, bytes_accessed=16 * size, transcendentals=2 * size
        ),
        name="update",
    )(
        place,
        *row_blocks,
        signs,
        pltpu.with_memory_space_constraint(weight, pltpu.HBM),
        pltpu.with_memory_space_constraint(second, pltpu.HBM),
        *onto,
    )


CORE, X, Y, Z0, Z1 = 1, 2, 4, 8, 16


def exchange(value, mask):
    size = lax.axis_size("dp") * lax.axis_size("col")
    return lax.ppermute(value, AXES, [(i, i ^ mask) for i in range(size)])


def stepped(tokens, out_grad, weight, second, momentum, sign_seed, step_number):
    low_rank = momentum.shape[1]
    owner_rows = momentum.shape[0]
    total_tokens = lax.axis_size("dp") * tokens.shape[0]
    inv_root = 1.0 / jnp.sqrt(jnp.float32(low_rank))
    place = jnp.stack(
        [lax.axis_index("col").astype(jnp.int32), sign_seed[0], step_number[0]]
    )

    far0 = [(Z1 | X | Z0, 0), (Z1 | X, 0), (Z1 | Z0, 0), (Z1, 0)]
    near0 = [(Z0 | X, 0), (X, 0), (Z0, 0), (0, 0)]
    far1 = [(Z1 | Y | X, 1), (Z1 | Y, 1), (Z1 | X, 1), (Z1, 1)]
    near1 = [(Y | X, 1), (Y, 1), (X, 1), (0, 1)]

    def toward(mask, pieces):
        return [(rel ^ mask, half) for rel, half in pieces]

    part = owner_rows // 2
    over_y, over_z = far0 + near0, far1 + near1
    og_y, og_z = pack(out_grad, [toward(Y, over_y), toward(Z0, over_z)], owner_rows, part)
    og_y = exchange(og_y, Y)
    og_z = exchange(og_z, Z0)
    signs, send_a, keep_a = sketch_parts(place, tokens, low_rank, None)
    og_yc, og_zc, og_c, og_own = pack(
        out_grad,
        [
            toward(Y | CORE, over_y),
            toward(Z0 | CORE, over_z),
            toward(CORE, over_y + over_z),
            over_y + over_z,
        ],
        owner_rows,
        part,
    )
    got_a = exchange(send_a, CORE)
    across = exchange(keep_a + got_a, X)
    og_yc = exchange(og_yc, Y | CORE)
    og_zc = exchange(og_zc, Z0 | CORE)
    og_c = exchange(og_c, CORE)
    send_b, keep_b = sketch_parts(place, tokens, low_rank, signs)
    got_b = exchange(send_b, CORE)
    sketch = (((keep_b + got_b) + across) * inv_root).astype(jnp.bfloat16)

    sk_y = exchange(sketch, Y)
    sk_z = exchange(sketch, Z0)
    sk_c = exchange(sketch, CORE)
    sk_yc = exchange(sk_y, CORE)
    sk_zc = exchange(sk_z, CORE)

    scale = jnp.float32(1.0 / total_tokens)

    def packed(value, extra):
        return (value * (scale * extra)).astype(jnp.float16)

    def unpacked(value, extra):
        return value.astype(jnp.float32) * (1.0 / (scale * extra))

    y_side = (sketch, sk_c, sk_y, sk_yc), (og_own, og_c, og_y, og_yc)
    z_side = (sketch, sk_c, sk_z, sk_zc), (og_own, og_c, og_z, og_zc)

    def begin(side, offsets, axis):
        send, keep = project(*side, offsets, 4)
        return exchange(packed(send, 8.0), axis), keep

    def middle(state, axis):
        got, keep = state
        ahead = exchange(packed(keep[0] + unpacked(got[0], 8.0), 4.0), axis)
        return ahead, keep[1] + unpacked(got[1], 8.0)

    def finish(state):
        got, keep = state
        return keep + unpacked(got, 4.0)

    far0_state = begin(y_side, (0, 0, 0, 0), X)
    far1_state = begin(z_side, (8, 8, 0, 0), Y)
    near0_state = begin(y_side, (4, 4, 4, 4), X)
    near1_state = begin(z_side, (12, 12, 4, 4), Y)
    far0_state = middle(far0_state, Z0)
    far1_state = middle(far1_state, X)
    last0 = exchange(packed(finish(far0_state), 2.0), Z1)
    last1 = exchange(packed(finish(far1_state), 2.0), Z1)
    near0_state = middle(near0_state, Z0)
    near1_state = middle(near1_state, X)

    def momentum_half(half, near, last):
        projected = (near + unpacked(last, 2.0)) * scale
        return 0.8 * momentum[half * part : (half + 1) * part] + 0.2 * projected

    halves, pieces = [], []
    small = None
    for half, near_state, last in ((0, near0_state, last0), (1, near1_state, last1)):
        if small is not None:
            last, _ = lax.optimization_barrier((last, small))
        mine = momentum_half(half, finish(near_state), last)
        small = mine.astype(jnp.float16)
        from_core = exchange(small, CORE)
        from_x = exchange(small, X)
        from_xc = exchange(from_x, CORE)
        halves.append(mine)
        pieces.append([v.astype(jnp.float32) for v in (from_core, from_x, from_xc)])
    done = ()
    for half in (0, 1):
        rows = (halves[half], pieces[half][0])
        done = update(place, rows, (0, CORE), half, signs, weight, second, tuple(done))
    for half in (0, 1):
        rows = (pieces[half][1], pieces[half][2])
        done = update(place, rows, (X, X | CORE), half, signs, weight, second, tuple(done))
    return (done[0], done[1], jnp.concatenate(halves, axis=0))


def solution(mesh):
    placed = (
        P("dp", "col"),
        P(AXES, None),
        P("dp", "col"),
        P("dp", "col"),
        P(AXES, None),
        P(),
        P(),
    )

    def per_device(tokens, out_grad, weight, second, momentum, sign_seed, step_number):
        args = (tokens, out_grad, weight, second, momentum, sign_seed, step_number)
        cube = mesh.shape["dp"] == Z1 * 2 // (X * 2) and mesh.shape["col"] == X * 2
        if cube and momentum.shape[0] % (2 * LANES) == 0:
            return stepped(*args)
        return general(*args)

    return jax.shard_map(
        per_device,
        mesh=mesh,
        in_specs=placed,
        out_specs=(P("dp", "col"), P("dp", "col"), P(AXES, None)),
        check_vma=False,
    )
```

profile of v0, /device:TPU:0, one launch (start us, length us, event | category | flops | bytes accessed | tf_op | source)
XLA Modules:
  0.0 136.1 jit_solution(9031084470028487406)
XLA Ops:
  2.0 2.2 %copy-done = bf16[1024,2048]{1,0:T(8,128)(2,1)S(1)} copy-done((bf16[1024,2048]{1,0:T(8,128)(2,1)S(1)}, bf16[1024,2048]{1,0:T(8,128)(2,1)}, u32[]{:S(2)}) %copy-start) | copy-done | bytes 4194328
  4.2 4.9 %sketch_first.1 = (bf16[2048,512]{1,0:T(8,128)(2,1)S(1)}, f32[256,512]{1,0:T(8,128)S(1)}, f32[256,512]{1,0:T(8,128)S(1)}) custom-call(s32[3]{0:T(128)S(1)} %pad_add_fusion.place_ref, bf16[1024,2048]{1,0:T(8,128)(2,1)S(1)} %copy-done), custom_call_target="tpu_custom_call" | custom-call | flops 1073741824 | bytes 6291456 | tf_op jit(solution)/shard_map/sketch_first/pallas_call | solution.py:218
  9.1 0.6 collective-permute-start.1
  9.6 3.0 %sketch_next.1 = (f32[256,512]{1,0:T(8,128)S(1)}, f32[256,512]{1,0:T(8,128)S(1)}) custom-call(s32[3]{0:T(128)S(1)} %pad_add_fusion.place_ref, bf16[1024,2048]{1,0:T(8,128)(2,1)S(1)} %copy-done, bf16[2048,512]{1,0:T(8,128)(2,1)S(1)} %get-tuple-element.31.signs_ref.refs_2_), custom_call_target="tpu_custom_call" | custom-call | flops 1073741824 | bytes 6291456 | tf_op jit(solution)/shard_map/sketch_next/pallas_call | solution.py:218
  12.8 3.0 %collective-permute-start.2 = (f32[256,512]{1,0:T(8,128)S(1)}, f32[256,512]{1,0:T(8,128)S(1)}, u32[]{:S(2)}, u32[]{:S(2)}) collective-permute-start(f32[256,512]{1,0:T(8,128)S(1)} %add.74), channel_id=1, source_target_pairs={{0,2},{1,3},{2,0},{3,1},{4,6},{5,7},{6,4},{7,5},{8,10},{9,11},{10,... | collective-permute-start | bytes 1572872 | tf_op jit(solution)/shard_map/ppermute | solution.py:372
  15.8 2.5 %pack.2 = (bf16[8,256,128]{2,1,0:T(8,128)(2,1)S(1)}, bf16[8,256,128]{2,1,0:T(8,128)(2,1)S(1)}, bf16[16,256,128]{2,1,0:T(8,128)(2,1)S(1)}, bf16[16,256,128]{2,1,0:T(8,128)(2,1)S(1)}) custom-call(bf16[256,8192]{1,0:T(8,128)(2,1)} %og_ref.3), custom_call_target="tpu_custom_call" | custom-call | bytes 6291456 | tf_op jit(solution)/shard_map/pack/pallas_call | solution.py:126
  18.4 1.6 %collective-permute-start.17 = (bf16[8,256,128]{2,1,0:T(8,128)(2,1)S(1)}, bf16[8,256,128]{2,1,0:T(8,128)(2,1)S(1)}, u32[]{:S(2)}, u32[]{:S(2)}) collective-permute-start(bf16[8,256,128]{2,1,0:T(8,128)(2,1)S(1)} %get-tuple-element.45), channel_id=1, source_target_pairs={{0,5},{1,4},{2,7},{3,6},{4,1},{5,0},{6,3},{7,2},{8,13},{9,12},{10,... | collective-permute-start | bytes 1572872 | tf_op jit(solution)/shard_map/ppermute | solution.py:372
  20.0 1.6 %pack.3 = (bf16[8,256,128]{2,1,0:T(8,128)(2,1)S(1)}, bf16[8,256,128]{2,1,0:T(8,128)(2,1)S(1)}) custom-call(bf16[256,8192]{1,0:T(8,128)(2,1)} %og_ref.3), custom_call_target="tpu_custom_call" | custom-call | bytes 2097152 | tf_op jit(solution)/shard_map/pack/pallas_call | solution.py:126
  21.7 0.6 collective-permute-start.16
  22.2 5.7 %collective-permute-done.2 = f32[256,512]{1,0:T(8,128)S(1)} collective-permute-done((f32[256,512]{1,0:T(8,128)S(1)}, f32[256,512]{1,0:T(8,128)S(1)}, u32[]{:S(2)}, u32[]{:S(2)}) %collective-permute-start.2) | collective-permute-done | bytes 524320 | tf_op jit(solution)/shard_map/ppermute | solution.py:372
  28.1 1.8 %collective-permute-start.14 = (bf16[256,512]{1,0:T(8,128)(2,1)S(1)}, bf16[256,512]{1,0:T(8,128)(2,1)S(1)}, u32[]{:S(2)}, u32[]{:S(2)}) collective-permute-start(bf16[256,512]{1,0:T(8,128)(2,1)S(1)} %multiply_convert_fusion.4.refs_0_), channel_id=1, source_target_pairs={{0,4},{1,5},{2,6},{3,7},{4,0},{5,1},{6,2},{7,3},{8,12},{9,13},{10,... | collective-permute-start | bytes 786440 | tf_op jit(solution)/shard_map/ppermute | solution.py:372
  29.9 1.6 %collective-permute-start.4 = (bf16[256,512]{1,0:T(8,128)(2,1)S(1)}, bf16[256,512]{1,0:T(8,128)(2,1)S(1)}, u32[]{:S(2)}, u32[]{:S(2)}) collective-permute-start(bf16[256,512]{1,0:T(8,128)(2,1)S(1)} %multiply_convert_fusion.4.refs_0_), channel_id=1, source_target_pairs={{0,8},{1,9},{2,10},{3,11},{4,12},{5,13},{6,14},{7,15},{8,0},{9,1},... | collective-permute-start | bytes 786440 | tf_op jit(solution)/shard_map/ppermute | solution.py:372
  31.5 0.8 collective-permute-done.17.refs_7_
  32.3 0.8 collective-permute-start.3
  33.1 16.4 %collective-permute-done.14.refs_2_ = bf16[256,512]{1,0:T(8,128)(2,1)S(1)} collective-permute-done((bf16[256,512]{1,0:T(8,128)(2,1)S(1)}, bf16[256,512]{1,0:T(8,128)(2,1)S(1)}, u32[]{:S(2)}, u32[]{:S(2)}) %collective-permute-start.14) | collective-permute-done | bytes 262176 | tf_op jit(solution)/shard_map/ppermute | solution.py:372
  49.6 1.7 %collective-permute-start.8 = (bf16[8,256,128]{2,1,0:T(8,128)(2,1)S(1)}, bf16[8,256,128]{2,1,0:T(8,128)(2,1)S(1)}, u32[]{:S(2)}, u32[]{:S(2)}) collective-permute-start(bf16[8,256,128]{2,1,0:T(8,128)(2,1)S(1)} %get-tuple-element.39), channel_id=1, source_target_pairs={{0,9},{1,8},{2,11},{3,10},{4,13},{5,12},{6,15},{7,14},{8,1},{9,0},... | collective-permute-start | bytes 1572872 | tf_op jit(solution)/shard_map/ppermute | solution.py:372
  51.2 0.5 collective-permute-start.7
  51.7 0.7 project.6
  52.5 0.4 collective-permute-start.18
  52.9 0.7 project.7
  53.7 1.8 %collective-permute-start.20 = (f16[2,128,512]{2,1,0:T(8,128)(2,1)S(1)}, f16[2,128,512]{2,1,0:T(8,128)(2,1)S(1)}, u32[]{:S(2)}, u32[]{:S(2)}) collective-permute-start(f16[2,128,512]{2,1,0:T(8,128)(2,1)S(1)} %multiply_convert_fusion), channel_id=1, source_target_pairs={{0,2},{1,3},{2,0},{3,1},{4,6},{5,7},{6,4},{7,5},{8,10},{9,11},{10,... | collective-permute-start | bytes 786440 | tf_op jit(solution)/shard_map/ppermute | solution.py:372
  55.5 8.1 %collective-permute-done.8.refs_7_ = bf16[8,256,128]{2,1,0:T(8,128)(2,1)S(1)} collective-permute-done((bf16[8,256,128]{2,1,0:T(8,128)(2,1)S(1)}, bf16[8,256,128]{2,1,0:T(8,128)(2,1)S(1)}, u32[]{:S(2)}, u32[]{:S(2)}) %collective-permute-start.8) | collective-permute-done | bytes 524320 | tf_op jit(solution)/shard_map/ppermute | solution.py:372
  63.6 11.5 %collective-permute-done.7.refs_6_ = bf16[8,256,128]{2,1,0:T(8,128)(2,1)S(1)} collective-permute-done((bf16[8,256,128]{2,1,0:T(8,128)(2,1)S(1)}, bf16[8,256,128]{2,1,0:T(8,128)(2,1)S(1)}, u32[]{:S(2)}, u32[]{:S(2)}) %collective-permute-start.7) | collective-permute-done | bytes 524320 | tf_op jit(solution)/shard_map/ppermute | solution.py:372
  75.0 0.7 project.4
  75.8 1.6 %collective-permute-start.9 = (f16[2,128,512]{2,1,0:T(8,128)(2,1)S(1)}, f16[2,128,512]{2,1,0:T(8,128)(2,1)S(1)}, u32[]{:S(2)}, u32[]{:S(2)}) collective-permute-start(f16[2,128,512]{2,1,0:T(8,128)(2,1)S(1)} %multiply_convert_fusion.3), channel_id=1, source_target_pairs={{0,4},{1,5},{2,6},{3,7},{4,0},{5,1},{6,2},{7,3},{8,12},{9,13},{10,... | collective-permute-start | bytes 786440 | tf_op jit(solution)/shard_map/ppermute | solution.py:372
  77.4 0.7 project.5
  78.2 0.6 collective-permute-start.11
  78.8 1.6 %collective-permute-start.19 = (f16[128,512]{1,0:T(8,128)(2,1)S(1)}, f16[128,512]{1,0:T(8,128)(2,1)S(1)}, u32[]{:S(2)}, u32[]{:S(2)}) collective-permute-start(f16[128,512]{1,0:T(8,128)(2,1)S(1)} %fusion.12), channel_id=1, source_target_pairs={{0,8},{1,9},{2,10},{3,11},{4,12},{5,13},{6,14},{7,15},{8,0},{9,1},... | collective-permute-start | bytes 393224 | tf_op jit(solution)/shard_map/ppermute | solution.py:372
  80.5 0.5 collective-permute-start.21
  81.0 4.0 %collective-permute-done.9 = f16[2,128,512]{2,1,0:T(8,128)(2,1)S(1)} collective-permute-done((f16[2,128,512]{2,1,0:T(8,128)(2,1)S(1)}, f16[2,128,512]{2,1,0:T(8,128)(2,1)S(1)}, u32[]{:S(2)}, u32[]{:S(2)}) %collective-permute-start.9) | collective-permute-done | bytes 262176 | tf_op jit(solution)/shard_map/ppermute | solution.py:372
  85.1 0.5 collective-permute-start.10
  85.7 3.5 %collective-permute-done.11 = f16[2,128,512]{2,1,0:T(8,128)(2,1)S(1)} collective-permute-done((f16[2,128,512]{2,1,0:T(8,128)(2,1)S(1)}, f16[2,128,512]{2,1,0:T(8,128)(2,1)S(1)}, u32[]{:S(2)}, u32[]{:S(2)}) %collective-permute-start.11) | collective-permute-done | bytes 262176 | tf_op jit(solution)/shard_map/ppermute | solution.py:372
  89.2 0.7 collective-permute-start.12
  90.0 2.6 %collective-permute-start.22 = (f16[128,512]{1,0:T(8,128)(2,1)S(1)}, f16[128,512]{1,0:T(8,128)(2,1)S(1)}, u32[]{:S(2)}, u32[]{:S(2)}) collective-permute-start(f16[128,512]{1,0:T(8,128)(2,1)S(1)} %fusion.1), channel_id=1, source_target_pairs={{0,16},{1,17},{2,18},{3,19},{4,20},{5,21},{6,22},{7,23},{8,24},{9,... | collective-permute-start | bytes 393224 | tf_op jit(solution)/shard_map/ppermute | solution.py:372
  92.5 1.7 %collective-permute-done.12 = f16[128,512]{1,0:T(8,128)(2,1)S(1)} collective-permute-done((f16[128,512]{1,0:T(8,128)(2,1)S(1)}, f16[128,512]{1,0:T(8,128)(2,1)S(1)}, u32[]{:S(2)}, u32[]{:S(2)}) %collective-permute-start.12) | collective-permute-done | bytes 131104 | tf_op jit(solution)/shard_map/ppermute | solution.py:372
  94.3 2.6 %collective-permute-start.13 = (f16[128,512]{1,0:T(8,128)(2,1)S(1)}, f16[128,512]{1,0:T(8,128)(2,1)S(1)}, u32[]{:S(2)}, u32[]{:S(2)}) collective-permute-start(f16[128,512]{1,0:T(8,128)(2,1)S(1)} %fusion.6), channel_id=1, source_target_pairs={{0,16},{1,17},{2,18},{3,19},{4,20},{5,21},{6,22},{7,23},{8,24},{9,... | collective-permute-start | bytes 393224 | tf_op jit(solution)/shard_map/ppermute | solution.py:372
  97.0 2.9 %collective-permute-done.22 = f16[128,512]{1,0:T(8,128)(2,1)S(1)} collective-permute-done((f16[128,512]{1,0:T(8,128)(2,1)S(1)}, f16[128,512]{1,0:T(8,128)(2,1)S(1)}, u32[]{:S(2)}, u32[]{:S(2)}) %collective-permute-start.22) | collective-permute-done | bytes 131104 | tf_op jit(solution)/shard_map/ppermute | solution.py:372
  100.1 3.1 %collective-permute-start.25 = (f16[128,512]{1,0:T(8,128)(2,1)S(1)}, f16[128,512]{1,0:T(8,128)(2,1)S(1)}, u32[]{:S(2)}, u32[]{:S(2)}) collective-permute-start(f16[128,512]{1,0:T(8,128)(2,1)S(1)} %get-tuple-element.61), channel_id=1, source_target_pairs={{0,2},{1,3},{2,0},{3,1},{4,6},{5,7},{6,4},{7,5},{8,10},{9,11},{10,... | collective-permute-start | bytes 393224 | tf_op jit(solution)/shard_map/ppermute | solution.py:372
  103.3 0.2 collective-permute-start.27
  103.6 1.2 collective-permute-start.23
  104.7 0.8 pad_maximum_fusion
  105.6 2.0 %collective-permute-done.25 = f16[128,512]{1,0:T(8,128)(2,1)S(1)} collective-permute-done((f16[128,512]{1,0:T(8,128)(2,1)S(1)}, f16[128,512]{1,0:T(8,128)(2,1)S(1)}, u32[]{:S(2)}, u32[]{:S(2)}) %collective-permute-start.25) | collective-permute-done | bytes 131104 | tf_op jit(solution)/shard_map/ppermute | solution.py:372
  107.5 6.9 %update.4 = (f32[1024,2048]{1,0:T(8,128)}, f32[1024,2048]{1,0:T(8,128)}) custom-call(s32[3]{0:T(128)S(1)} %pad_add_fusion.place_ref, f32[128,512]{1,0:T(8,128)S(1)} %get-tuple-element.62.refs_0_, f32[128,512]{1,0:T(8,128)S(1)} %convert_element_type.127.refs_1_, bf16[2048,512]{1,0:T(8,128)(2,1)S(1)} %get-tuple-element.31.signs_ref.refs_2_, ...), custom_call_target="tpu_custom_call" | custom-call | flops 1073741824 | bytes 8388608 | tf_op jit(solution)/shard_map/update/pallas_call | solution.py:341
  114.5 0.6 collective-permute-start.24
  115.0 6.8 %update.5 = (f32[1024,2048]{1,0:T(8,128)}, f32[1024,2048]{1,0:T(8,128)}) custom-call(s32[3]{0:T(128)S(1)} %pad_add_fusion.place_ref, f32[128,512]{1,0:T(8,128)S(1)} %get-tuple-element.60.refs_0_, f32[128,512]{1,0:T(8,128)S(1)} %convert_element_type.126.refs_1_, ...), custom_call_target="tpu_custom_call", output_to_operand_aliasing={{0}: (6, {}), {1}: (7, {})} | custom-call | flops 1073741824 | bytes 8388608 | tf_op jit(solution)/shard_map/update/pallas_call | solution.py:341
  122.0 0.2 convert_element_type.125.refs_1_
  122.2 6.9 %update.6 = (f32[1024,2048]{1,0:T(8,128)}, f32[1024,2048]{1,0:T(8,128)}) custom-call(s32[3]{0:T(128)S(1)} %pad_add_fusion.place_ref, f32[128,512]{1,0:T(8,128)S(1)} %convert_element_type.124.refs_0_, f32[128,512]{1,0:T(8,128)S(1)} %convert_element_type.125.refs_1_, ...), custom_call_target="tpu_custom_call", output_to_operand_aliasing={{0}: (6, {}), {1}: (7, {})} | custom-call | flops 1073741824 | bytes 8388608 | tf_op jit(solution)/shard_map/update/pallas_call | solution.py:341
  129.1 6.9 %update.7 = (f32[1024,2048]{1,0:T(8,128)}, f32[1024,2048]{1,0:T(8,128)}) custom-call(s32[3]{0:T(128)S(1)} %pad_add_fusion.place_ref, f32[128,512]{1,0:T(8,128)S(1)} %convert_element_type.122.refs_0_, f32[128,512]{1,0:T(8,128)S(1)} %convert_element_type.123.refs_1_, ...), custom_call_target="tpu_custom_call", output_to_operand_aliasing={{0}: (6, {}), {1}: (7, {})} | custom-call | flops 1073741824 | bytes 8388608 | tf_op jit(solution)/shard_map/update/pallas_call | solution.py:341
  (48 shorter events, 1.6 us)
Async XLA Ops:
  2.0 2.2 %copy-start = (bf16[1024,2048]{1,0:T(8,128)(2,1)S(1)}, bf16[1024,2048]{1,0:T(8,128)(2,1)}, u32[]{:S(2)}) copy-start(bf16[1024,2048]{1,0:T(8,128)(2,1)} %tok_ref.3) | copy-start | bytes 12582916
  9.1 3.6 %collective-permute-start.1 = (f32[256,512]{1,0:T(8,128)S(1)}, f32[256,512]{1,0:T(8,128)S(1)}, u32[]{:S(2)}, u32[]{:S(2)}) collective-permute-start(f32[256,512]{1,0:T(8,128)S(1)} %get-tuple-element.35), channel_id=1, source_target_pairs={{0,1},{1,0},{2,3},{3,2},{4,5},{5,4},{6,7},{7,6},{8,9},{9,8},{10,11... | collective-permute-start | bytes 1572872 | tf_op jit(solution)/shard_map/ppermute | solution.py:372
  12.6 9.6 %collective-permute-start = (f32[256,512]{1,0:T(8,128)S(1)}, f32[256,512]{1,0:T(8,128)S(1)}, u32[]{:S(2)}, u32[]{:S(2)}) collective-permute-start(f32[256,512]{1,0:T(8,128)S(1)} %get-tuple-element.33), channel_id=1, source_target_pairs={{0,1},{1,0},{2,3},{3,2},{4,5},{5,4},{6,7},{7,6},{8,9},{9,8},{10,11... | collective-permute-start | bytes 1572872 | tf_op jit(solution)/shard_map/ppermute | solution.py:372
  12.8 15.1 %collective-permute-start.2 = (f32[256,512]{1,0:T(8,128)S(1)}, f32[256,512]{1,0:T(8,128)S(1)}, u32[]{:S(2)}, u32[]{:S(2)}) collective-permute-start(f32[256,512]{1,0:T(8,128)S(1)} %add.74), channel_id=1, source_target_pairs={{0,2},{1,3},{2,0},{3,1},{4,6},{5,7},{6,4},{7,5},{8,10},{9,11},{10,... | collective-permute-start | bytes 1572872 | tf_op jit(solution)/shard_map/ppermute | solution.py:372
  18.3 32.9 %collective-permute-start.6 = (bf16[16,256,128]{2,1,0:T(8,128)(2,1)S(1)}, bf16[16,256,128]{2,1,0:T(8,128)(2,1)S(1)}, u32[]{:S(2)}, u32[]{:S(2)}) collective-permute-start(bf16[16,256,128]{2,1,0:T(8,128)(2,1)S(1)} %get-tuple-element.37), channel_id=1, source_target_pairs={{0,1},{1,0},{2,3},{3,2},{4,5},{5,4},{6,7},{7,6},{8,9},{9,8},{10,11... | collective-permute-start | bytes 3145736 | tf_op jit(solution)/shard_map/ppermute | solution.py:372
  18.4 13.9 %collective-permute-start.17 = (bf16[8,256,128]{2,1,0:T(8,128)(2,1)S(1)}, bf16[8,256,128]{2,1,0:T(8,128)(2,1)S(1)}, u32[]{:S(2)}, u32[]{:S(2)}) collective-permute-start(bf16[8,256,128]{2,1,0:T(8,128)(2,1)S(1)} %get-tuple-element.45), channel_id=1, source_target_pairs={{0,5},{1,4},{2,7},{3,6},{4,1},{5,0},{6,3},{7,2},{8,13},{9,12},{10,... | collective-permute-start | bytes 1572872 | tf_op jit(solution)/shard_map/ppermute | solution.py:372
  21.7 27.9 %collective-permute-start.16 = (bf16[8,256,128]{2,1,0:T(8,128)(2,1)S(1)}, bf16[8,256,128]{2,1,0:T(8,128)(2,1)S(1)}, u32[]{:S(2)}, u32[]{:S(2)}) collective-permute-start(bf16[8,256,128]{2,1,0:T(8,128)(2,1)S(1)} %get-tuple-element.44), channel_id=1, source_target_pairs={{0,4},{1,5},{2,6},{3,7},{4,0},{5,1},{6,2},{7,3},{8,12},{9,13},{10,... | collective-permute-start | bytes 1572872 | tf_op jit(solution)/shard_map/ppermute | solution.py:372
  28.1 21.4 %collective-permute-start.14 = (bf16[256,512]{1,0:T(8,128)(2,1)S(1)}, bf16[256,512]{1,0:T(8,128)(2,1)S(1)}, u32[]{:S(2)}, u32[]{:S(2)}) collective-permute-start(bf16[256,512]{1,0:T(8,128)(2,1)S(1)} %multiply_convert_fusion.4.refs_0_), channel_id=1, source_target_pairs={{0,4},{1,5},{2,6},{3,7},{4,0},{5,1},{6,2},{7,3},{8,12},{9,13},{10,... | collective-permute-start | bytes 786440 | tf_op jit(solution)/shard_map/ppermute | solution.py:372
  29.9 21.8 %collective-permute-start.4 = (bf16[256,512]{1,0:T(8,128)(2,1)S(1)}, bf16[256,512]{1,0:T(8,128)(2,1)S(1)}, u32[]{:S(2)}, u32[]{:S(2)}) collective-permute-start(bf16[256,512]{1,0:T(8,128)(2,1)S(1)} %multiply_convert_fusion.4.refs_0_), channel_id=1, source_target_pairs={{0,8},{1,9},{2,10},{3,11},{4,12},{5,13},{6,14},{7,15},{8,0},{9,1},... | collective-permute-start | bytes 786440 | tf_op jit(solution)/shard_map/ppermute | solution.py:372
  32.3 19.4 %collective-permute-start.3 = (bf16[256,512]{1,0:T(8,128)(2,1)S(1)}, bf16[256,512]{1,0:T(8,128)(2,1)S(1)}, u32[]{:S(2)}, u32[]{:S(2)}) collective-permute-start(bf16[256,512]{1,0:T(8,128)(2,1)S(1)} %multiply_convert_fusion.4.refs_0_), channel_id=1, source_target_pairs={{0,1},{1,0},{2,3},{3,2},{4,5},{5,4},{6,7},{7,6},{8,9},{9,8},{10,11... | collective-permute-start | bytes 786440 | tf_op jit(solution)/shard_map/ppermute | solution.py:372
  49.5 2.2 %collective-permute-start.15 = (bf16[256,512]{1,0:T(8,128)(2,1)S(1)}, bf16[256,512]{1,0:T(8,128)(2,1)S(1)}, u32[]{:S(2)}, u32[]{:S(2)}) collective-permute-start(bf16[256,512]{1,0:T(8,128)(2,1)S(1)} %collective-permute-done.14.refs_2_), channel_id=1, source_target_pairs={{0,1},{1,0},{2,3},{3,2},{4,5},{5,4},{6,7},{7,6},{8,9},{9,8},{10,11... | collective-permute-start | bytes 786440 | tf_op jit(solution)/shard_map/ppermute | solution.py:372
  49.6 14.0 %collective-permute-start.8 = (bf16[8,256,128]{2,1,0:T(8,128)(2,1)S(1)}, bf16[8,256,128]{2,1,0:T(8,128)(2,1)S(1)}, u32[]{:S(2)}, u32[]{:S(2)}) collective-permute-start(bf16[8,256,128]{2,1,0:T(8,128)(2,1)S(1)} %get-tuple-element.39), channel_id=1, source_target_pairs={{0,9},{1,8},{2,11},{3,10},{4,13},{5,12},{6,15},{7,14},{8,1},{9,0},... | collective-permute-start | bytes 1572872 | tf_op jit(solution)/shard_map/ppermute | solution.py:372
  51.2 23.8 %collective-permute-start.7 = (bf16[8,256,128]{2,1,0:T(8,128)(2,1)S(1)}, bf16[8,256,128]{2,1,0:T(8,128)(2,1)S(1)}, u32[]{:S(2)}, u32[]{:S(2)}) collective-permute-start(bf16[8,256,128]{2,1,0:T(8,128)(2,1)S(1)} %get-tuple-element.38), channel_id=1, source_target_pairs={{0,8},{1,9},{2,10},{3,11},{4,12},{5,13},{6,14},{7,15},{8,0},{9,1},... | collective-permute-start | bytes 1572872 | tf_op jit(solution)/shard_map/ppermute | solution.py:372
  51.7 23.3 %collective-permute-start.5 = (bf16[256,512]{1,0:T(8,128)(2,1)S(1)}, bf16[256,512]{1,0:T(8,128)(2,1)S(1)}, u32[]{:S(2)}, u32[]{:S(2)}) collective-permute-start(bf16[256,512]{1,0:T(8,128)(2,1)S(1)} %collective-permute-done.4.refs_2_), channel_id=1, source_target_pairs={{0,1},{1,0},{2,3},{3,2},{4,5},{5,4},{6,7},{7,6},{8,9},{9,8},{10,11... | collective-permute-start | bytes 786440 | tf_op jit(solution)/shard_map/ppermute | solution.py:372
  52.5 47.4 %copy-start.1 = (f32[256,512]{1,0:T(8,128)S(1)}, f32[256,512]{1,0:T(8,128)}, u32[]{:S(2)}) copy-start(f32[256,512]{1,0:T(8,128)} %param.11) | copy-start | bytes 1572868
  52.5 26.2 %collective-permute-start.18 = (f16[2,128,512]{2,1,0:T(8,128)(2,1)S(1)}, f16[2,128,512]{2,1,0:T(8,128)(2,1)S(1)}, u32[]{:S(2)}, u32[]{:S(2)}) collective-permute-start(f16[2,128,512]{2,1,0:T(8,128)(2,1)S(1)} %multiply_convert_fusion.1), channel_id=1, source_target_pairs={{0,2},{1,3},{2,0},{3,1},{4,6},{5,7},{6,4},{7,5},{8,10},{9,11},{10,... | collective-permute-start | bytes 786440 | tf_op jit(solution)/shard_map/ppermute | solution.py:372
  53.7 26.7 %collective-permute-start.20 = (f16[2,128,512]{2,1,0:T(8,128)(2,1)S(1)}, f16[2,128,512]{2,1,0:T(8,128)(2,1)S(1)}, u32[]{:S(2)}, u32[]{:S(2)}) collective-permute-start(f16[2,128,512]{2,1,0:T(8,128)(2,1)S(1)} %multiply_convert_fusion), channel_id=1, source_target_pairs={{0,2},{1,3},{2,0},{3,1},{4,6},{5,7},{6,4},{7,5},{8,10},{9,11},{10,... | collective-permute-start | bytes 786440 | tf_op jit(solution)/shard_map/ppermute | solution.py:372
  75.8 9.2 %collective-permute-start.9 = (f16[2,128,512]{2,1,0:T(8,128)(2,1)S(1)}, f16[2,128,512]{2,1,0:T(8,128)(2,1)S(1)}, u32[]{:S(2)}, u32[]{:S(2)}) collective-permute-start(f16[2,128,512]{2,1,0:T(8,128)(2,1)S(1)} %multiply_convert_fusion.3), channel_id=1, source_target_pairs={{0,4},{1,5},{2,6},{3,7},{4,0},{5,1},{6,2},{7,3},{8,12},{9,13},{10,... | collective-permute-start | bytes 786440 | tf_op jit(solution)/shard_map/ppermute | solution.py:372
  78.2 11.0 %collective-permute-start.11 = (f16[2,128,512]{2,1,0:T(8,128)(2,1)S(1)}, f16[2,128,512]{2,1,0:T(8,128)(2,1)S(1)}, u32[]{:S(2)}, u32[]{:S(2)}) collective-permute-start(f16[2,128,512]{2,1,0:T(8,128)(2,1)S(1)} %multiply_convert_fusion.2), channel_id=1, source_target_pairs={{0,4},{1,5},{2,6},{3,7},{4,0},{5,1},{6,2},{7,3},{8,12},{9,13},{10,... | collective-permute-start | bytes 786440 | tf_op jit(solution)/shard_map/ppermute | solution.py:372
  78.8 18.1 %collective-permute-start.19 = (f16[128,512]{1,0:T(8,128)(2,1)S(1)}, f16[128,512]{1,0:T(8,128)(2,1)S(1)}, u32[]{:S(2)}, u32[]{:S(2)}) collective-permute-start(f16[128,512]{1,0:T(8,128)(2,1)S(1)} %fusion.12), channel_id=1, source_target_pairs={{0,8},{1,9},{2,10},{3,11},{4,12},{5,13},{6,14},{7,15},{8,0},{9,1},... | collective-permute-start | bytes 393224 | tf_op jit(solution)/shard_map/ppermute | solution.py:372
  80.5 9.4 %collective-permute-start.21 = (f16[128,512]{1,0:T(8,128)(2,1)S(1)}, f16[128,512]{1,0:T(8,128)(2,1)S(1)}, u32[]{:S(2)}, u32[]{:S(2)}) collective-permute-start(f16[128,512]{1,0:T(8,128)(2,1)S(1)} %fusion.13), channel_id=1, source_target_pairs={{0,8},{1,9},{2,10},{3,11},{4,12},{5,13},{6,14},{7,15},{8,0},{9,1},... | collective-permute-start | bytes 393224 | tf_op jit(solution)/shard_map/ppermute | solution.py:372
  85.1 18.1 %collective-permute-start.10 = (f16[128,512]{1,0:T(8,128)(2,1)S(1)}, f16[128,512]{1,0:T(8,128)(2,1)S(1)}, u32[]{:S(2)}, u32[]{:S(2)}) collective-permute-start(f16[128,512]{1,0:T(8,128)(2,1)S(1)} %fusion.10), channel_id=1, source_target_pairs={{0,2},{1,3},{2,0},{3,1},{4,6},{5,7},{6,4},{7,5},{8,10},{9,11},{10,... | collective-permute-start | bytes 393224 | tf_op jit(solution)/shard_map/ppermute | solution.py:372
  89.2 5.0 %collective-permute-start.12 = (f16[128,512]{1,0:T(8,128)(2,1)S(1)}, f16[128,512]{1,0:T(8,128)(2,1)S(1)}, u32[]{:S(2)}, u32[]{:S(2)}) collective-permute-start(f16[128,512]{1,0:T(8,128)(2,1)S(1)} %fusion.11), channel_id=1, source_target_pairs={{0,2},{1,3},{2,0},{3,1},{4,6},{5,7},{6,4},{7,5},{8,10},{9,11},{10,... | collective-permute-start | bytes 393224 | tf_op jit(solution)/shard_map/ppermute | solution.py:372
  90.0 9.9 %collective-permute-start.22 = (f16[128,512]{1,0:T(8,128)(2,1)S(1)}, f16[128,512]{1,0:T(8,128)(2,1)S(1)}, u32[]{:S(2)}, u32[]{:S(2)}) collective-permute-start(f16[128,512]{1,0:T(8,128)(2,1)S(1)} %fusion.1), channel_id=1, source_target_pairs={{0,16},{1,17},{2,18},{3,19},{4,20},{5,21},{6,22},{7,23},{8,24},{9,... | collective-permute-start | bytes 393224 | tf_op jit(solution)/shard_map/ppermute | solution.py:372
  94.3 8.9 %collective-permute-start.13 = (f16[128,512]{1,0:T(8,128)(2,1)S(1)}, f16[128,512]{1,0:T(8,128)(2,1)S(1)}, u32[]{:S(2)}, u32[]{:S(2)}) collective-permute-start(f16[128,512]{1,0:T(8,128)(2,1)S(1)} %fusion.6), channel_id=1, source_target_pairs={{0,16},{1,17},{2,18},{3,19},{4,20},{5,21},{6,22},{7,23},{8,24},{9,... | collective-permute-start | bytes 393224 | tf_op jit(solution)/shard_map/ppermute | solution.py:372
  100.0 5.6 %collective-permute-start.28 = (f16[128,512]{1,0:T(8,128)(2,1)S(1)}, f16[128,512]{1,0:T(8,128)(2,1)S(1)}, u32[]{:S(2)}, u32[]{:S(2)}) collective-permute-start(f16[128,512]{1,0:T(8,128)(2,1)S(1)} %get-tuple-element.61), channel_id=1, source_target_pairs={{0,1},{1,0},{2,3},{3,2},{4,5},{5,4},{6,7},{7,6},{8,9},{9,8},{10,11... | collective-permute-start | bytes 393224 | tf_op jit(solution)/shard_map/ppermute | solution.py:372
  100.1 7.5 %collective-permute-start.25 = (f16[128,512]{1,0:T(8,128)(2,1)S(1)}, f16[128,512]{1,0:T(8,128)(2,1)S(1)}, u32[]{:S(2)}, u32[]{:S(2)}) collective-permute-start(f16[128,512]{1,0:T(8,128)(2,1)S(1)} %get-tuple-element.61), channel_id=1, source_target_pairs={{0,2},{1,3},{2,0},{3,1},{4,6},{5,7},{6,4},{7,5},{8,10},{9,11},{10,... | collective-permute-start | bytes 393224 | tf_op jit(solution)/shard_map/ppermute | solution.py:372
  103.3 11.1 %collective-permute-start.27 = (f16[128,512]{1,0:T(8,128)(2,1)S(1)}, f16[128,512]{1,0:T(8,128)(2,1)S(1)}, u32[]{:S(2)}, u32[]{:S(2)}) collective-permute-start(f16[128,512]{1,0:T(8,128)(2,1)S(1)} %get-tuple-element.59), channel_id=1, source_target_pairs={{0,1},{1,0},{2,3},{3,2},{4,5},{5,4},{6,7},{7,6},{8,9},{9,8},{10,11... | collective-permute-start | bytes 393224 | tf_op jit(solution)/shard_map/ppermute | solution.py:372
  103.6 10.9 %collective-permute-start.23 = (f16[128,512]{1,0:T(8,128)(2,1)S(1)}, f16[128,512]{1,0:T(8,128)(2,1)S(1)}, u32[]{:S(2)}, u32[]{:S(2)}) collective-permute-start(f16[128,512]{1,0:T(8,128)(2,1)S(1)} %get-tuple-element.59), channel_id=1, source_target_pairs={{0,2},{1,3},{2,0},{3,1},{4,6},{5,7},{6,4},{7,5},{8,10},{9,11},{10,... | collective-permute-start | bytes 393224 | tf_op jit(solution)/shard_map/ppermute | solution.py:372
  107.5 14.4 %collective-permute-start.26 = (f16[128,512]{1,0:T(8,128)(2,1)S(1)}, f16[128,512]{1,0:T(8,128)(2,1)S(1)}, u32[]{:S(2)}, u32[]{:S(2)}) collective-permute-start(f16[128,512]{1,0:T(8,128)(2,1)S(1)} %collective-permute-done.25), channel_id=1, source_target_pairs={{0,1},{1,0},{2,3},{3,2},{4,5},{5,4},{6,7},{7,6},{8,9},{9,8},{10,11... | collective-permute-start | bytes 393224 | tf_op jit(solution)/shard_map/ppermute | solution.py:372
  114.5 14.6 %collective-permute-start.24 = (f16[128,512]{1,0:T(8,128)(2,1)S(1)}, f16[128,512]{1,0:T(8,128)(2,1)S(1)}, u32[]{:S(2)}, u32[]{:S(2)}) collective-permute-start(f16[128,512]{1,0:T(8,128)(2,1)S(1)} %collective-permute-done.23), channel_id=1, source_target_pairs={{0,1},{1,0},{2,3},{3,2},{4,5},{5,4},{6,7},{7,6},{8,9},{9,8},{10,11... | collective-permute-start | bytes 393224 | tf_op jit(solution)/shard_map/ppermute | solution.py:372
where the time goes:
time: 136 us
  waiting for transfers between devices  56.6 us (42%)
  Pallas kernels  42.3 us (31%)
  starting transfers between devices  30.3 us (22%)
  between operations  2.38 us (2%)
  other arithmetic  2.36 us (2%)
  local copies, waits for them, and re-layouts  2.2 us (2%)
    ppermute x29, waiting for transfers between devices, exchange(): return lax.ppermute(value, AXES, [(i, i ^ mask) for i in range(size)])  56.6 us
    ppermute x29, starting transfers between devices, exchange(): return lax.ppermute(value, AXES, [(i, i ^ mask) for i in range(size)])  30.3 us
    pallas_call x4, Pallas kernels, update(): pl.pallas_call(functools.partial(update_kernel, relatives, half), in_spec...  27.4 us
    pallas_call x2, Pallas kernels, sketch_parts(): pl.pallas_call(body, grid_spec=pltpu.PrefetchScalarGridSpec(num_scalar_pr...  7.83 us
    pallas_call x2, Pallas kernels, pack(): pl.pallas_call(functools.partial(pack_kernel, groups, width, part), in_sp...  4.14 us
    pallas_call x4, Pallas kernels, project(): pl.pallas_call(functools.partial(project_kernel, n), grid=(1,), in_specs=...  2.93 us
  transfers between devices with their start and end apart: 29, of which 10 were waited for; matrix products, arithmetic and copies ran while one was open for 2% of the time, Pallas kernels for 22%

commit v1 on v0

--- a/solution.py
+++ b/solution.py
@@ -1,4 +1,5 @@
 import functools
+import math
 
 import jax
 import jax.numpy as jnp
@@ -12,22 +13,21 @@
 LANES = 128
 
 
-def hashed_signs(flat_scaled, sign_seed, step_number):
-    hashed = flat_scaled + sign_seed * 1664525 + step_number * 1013904223
-    hashed = hashed ^ hashed >> 16 & 65535
-    hashed = hashed * 2127912213
-    hashed = hashed ^ hashed >> 13 & 524287
-    hashed = hashed * 1103515245
-    hashed = hashed ^ hashed >> 16 & 65535
-    return hashed >> 20 & 1
+def low_bits(mixed):
+    mixed = mixed ^ lax.shift_right_logical(mixed, 16)
+    mixed = mixed * 2127912213
+    mixed = mixed ^ lax.shift_right_logical(mixed, 13)
+    mixed = mixed * 1103515245
+    mixed = mixed ^ lax.shift_right_logical(mixed, 16)
+    return mixed & (1 << 20)
 
 
 def sign_table(sign_seed, step_number, first_row, row_count, low_rank):
     row_ids = first_row + lax.iota(jnp.int32, row_count)
     col_ids = lax.iota(jnp.int32, low_rank)
     flat_index = row_ids[:, None] * low_rank + col_ids[None, :]
-    low_bit = hashed_signs(flat_index * 747796405, sign_seed[0], step_number[0])
-    return (1 - 2 * low_bit).astype(jnp.float32)
+    seeded = sign_seed[0] * 1664525 + step_number[0] * 1013904223
+    return jnp.where(low_bits(flat_index * 747796405 + seeded) == 0, 1.0, -1.0)
 
 
 def contract(left_rows, right_rows):
@@ -135,7 +135,7 @@
             pltpu.SemaphoreType.DMA((count,)),
             pltpu.SemaphoreType.DMA((len(groups),)),
         ],
-        compiler_params=pltpu.CompilerParams(vmem_limit_bytes=16 * 1024 * 1024),
+        compiler_params=pltpu.CompilerParams(vmem_limit_bytes=8 * 1024 * 1024),
         cost_estimate=pl.CostEstimate(
             flops=0, bytes_accessed=4 * count * rows * part, transcendentals=0
         ),
@@ -143,96 +143,91 @@
     )(pltpu.with_memory_space_constraint(out_grad, pltpu.HBM))
 
 
-def split_acc(place_ref, acc, send_ref, keep_ref):
-    rows = keep_ref.shape[0]
-    core = place_ref[0] & 1
-    keep_ref[...] = acc[pl.ds(pl.multiple_of(core * rows, rows), rows), :]
-    send_ref[...] = acc[pl.ds(pl.multiple_of((1 - core) * rows, rows), rows), :]
-
-
-def sketch_first(steps, chunk, din_local, place_ref, tok_ref, signs_ref, send_ref, keep_ref, acc):
-    step = pl.program_id(0)
-    low_rank = signs_ref.shape[1]
-    shape = (chunk, low_rank)
-    first = place_ref[0] * din_local + step * chunk
-    flat = (first + lax.broadcasted_iota(jnp.int32, shape, 0)) * low_rank
-    flat = flat + lax.broadcasted_iota(jnp.int32, shape, 1)
-    low_bit = hashed_signs(flat * 747796405, place_ref[1], place_ref[2])
-    signs = jnp.where(low_bit == 1, -1.0, 1.0).astype(jnp.bfloat16)
-    signs_ref[...] = signs
-    part = jnp.dot(tok_ref[...], signs, preferred_element_type=jnp.float32)
-
-    @pl.when(step == 0)
-    def _():
-        acc[...] = part
-
-    @pl.when(step > 0)
-    def _():
-        acc[...] += part
-
-    @pl.when(step == steps - 1)
-    def _():
-        split_acc(place_ref, acc, send_ref, keep_ref)
-
-
-def sketch_next(steps, place_ref, tok_ref, signs_ref, send_ref, keep_ref, acc):
-    step = pl.program_id(0)
-    part = jnp.dot(tok_ref[...], signs_ref[...], preferred_element_type=jnp.float32)
-
-    @pl.when(step == 0)
-    def _():
-        acc[...] = part
-
-    @pl.when(step > 0)
-    def _():
-        acc[...] += part
-
-    @pl.when(step == steps - 1)
-    def _():
-        split_acc(place_ref, acc, send_ref, keep_ref)
-
-
-def sketch_parts(place, tokens, low_rank, signs):
+CHUNKS = 4
+
+
+def sketch_kernel(first, din_local, *refs):
+    if first:
+        seed_ref, step_ref, tok_ref, signs_ref, send_ref, keep_ref, tok, acc, sem = refs
+    else:
+        tok_ref, signs_ref, send_ref, keep_ref, tok, acc, sem = refs
+    quarter, low_rank = keep_ref.shape
+    chunk = din_local // CHUNKS
+    col = lax.axis_index("col")
+    group = col ^ (X if first else 0)
+    loads = []
+    for part in range(CHUNKS):
+        at = pl.ds(part * chunk, chunk)
+        mine = []
+        for slot, rel in enumerate((CORE, 0)):
+            rows = pl.ds(pl.multiple_of((group ^ rel) * quarter, quarter), quarter)
+            copy = pltpu.make_async_copy(
+                tok_ref.at[rows, at],
+                tok.at[pl.ds(slot * quarter, quarter), at],
+                sem.at[part, slot],
+            )
+            copy.start()
+            mine.append(copy)
+        loads.append(mine)
+    if first:
+        seeded = seed_ref[0] * 1664525 + step_ref[0] * 1013904223
+        columns = lax.broadcasted_iota(jnp.int32, (1, low_rank), 1) * 747796405
+    for part in range(CHUNKS):
+        at = slice(part * chunk, (part + 1) * chunk)
+        if first:
+            ids = lax.broadcasted_iota(jnp.int32, (chunk, 1), 0)
+            ids = (ids + (col * din_local + part * chunk)) * low_rank
+            mixed = (ids * 747796405 + seeded) + columns
+            signs = jnp.where(low_bits(mixed) == 0, 1.0, -1.0).astype(jnp.bfloat16)
+            signs_ref[at, :] = signs
+        else:
+            signs = signs_ref[at, :]
+        for copy in loads[part]:
+            copy.wait()
+        product = jnp.dot(tok[:, at], signs, preferred_element_type=jnp.float32)
+        if part > 0:
+            product += acc[...]
+        if part < CHUNKS - 1:
+            acc[...] = product
+        else:
+            send_ref[...] = product[:quarter]
+            keep_ref[...] = product[quarter:]
+
+
+def sketch_parts(tokens, low_rank, signs, seeds):
     local_tokens, din_local = tokens.shape
-    chunk = din_local // 4
-    steps = din_local // chunk
     half = local_tokens // 2
     quarter = half // 2
     first = signs is None
-    tok_spec = pl.BlockSpec(
-        (half, chunk), lambda i, p: ((p[0] >> 1) ^ (1 if first else 0), i)
-    )
-    sign_spec = pl.BlockSpec((chunk, low_rank), lambda i, p: (i, 0))
-    part_spec = pl.BlockSpec((quarter, low_rank), lambda i, p: (0, 0))
+    vmem = pl.BlockSpec(memory_space=pltpu.VMEM)
+    smem = pl.BlockSpec(memory_space=pltpu.SMEM)
+    hbm = pl.BlockSpec(memory_space=pl.ANY)
     parts = [jax.ShapeDtypeStruct((quarter, low_rank), jnp.float32)] * 2
+    tokens = pltpu.with_memory_space_constraint(tokens, pltpu.HBM)
     if first:
-        body = functools.partial(sketch_first, steps, chunk, din_local)
-        in_specs, args = [tok_spec], (tokens,)
-        out_specs = [sign_spec, part_spec, part_spec]
+        in_specs, args = [smem, smem, hbm], (*seeds, tokens)
         out_shape = [jax.ShapeDtypeStruct((din_local, low_rank), jnp.bfloat16)] + parts
     else:
-        body = functools.partial(sketch_next, steps)
-        in_specs, args = [tok_spec, sign_spec], (tokens, signs)
-        out_specs = [part_spec, part_spec]
+        in_specs, args = [hbm, vmem], (tokens, signs)
         out_shape = parts
     return pl.pallas_call(
-        body,
-        grid_spec=pltpu.PrefetchScalarGridSpec(
-            num_scalar_prefetch=1,
-            grid=(steps,),
-            in_specs=in_specs,
-            out_specs=out_specs,
-            scratch_shapes=[pltpu.VMEM((half, low_rank), jnp.float32)],
-        ),
+        functools.partial(sketch_kernel, first, din_local),
+        in_specs=in_specs,
+        out_specs=[vmem] * len(out_shape),
         out_shape=out_shape,
-        compiler_params=params(24 * 1024 * 1024),
+        scratch_shapes=[
+            pltpu.VMEM((half, din_local), tokens.dtype),
+            pltpu.VMEM((half, low_rank), jnp.float32),
+            pltpu.SemaphoreType.DMA((CHUNKS, 2)),
+        ],
+        compiler_params=pltpu.CompilerParams(vmem_limit_bytes=12 * 1024 * 1024),
         cost_estimate=pl.CostEstimate(
             flops=2 * half * din_local * low_rank,
             bytes_accessed=half * din_local * 2 + din_local * low_rank * 2 + 2 * half * low_rank * 4,
             transcendentals=0,
         ),
         name="sketch_first" if first else "sketch_next",
-    )(place, *args)
+    )(*args)
 
 
 def project_kernel(n, *refs):
@@ -268,7 +263,7 @@
         + [block_at(offset) for offset in offsets],
         out_specs=[pl.BlockSpec((count // 2, part, low_rank), lambda i: (0, 0, 0))] * 2,
         out_shape=[out] * 2,
-        compiler_params=params(16 * 1024 * 1024),
+        compiler_params=params(10 * 1024 * 1024),
         cost_estimate=pl.CostEstimate(
             flops=2 * n * count * rows * part * low_rank,
             bytes_accessed=n * (rows * low_rank + count * rows * part) * 2
@@ -279,89 +274,115 @@
     )(*sketches, *grads)
 
 
-def update_kernel(relatives, half, place_ref, *refs):
+def prefetch_kernel(*refs):
+    n = (len(refs) - 1) // 2
+    sources, targets, sem = refs[:n], refs[n : 2 * n], refs[-1]
+    pieces = sem.shape[1]
+    copies = []
+    for at in range(pieces):
+        for k, (source, target) in enumerate(zip(sources, targets)):
+            rows = source.shape[0] // pieces
+            window = pl.ds(at * rows, rows)
+            copy = pltpu.make_async_copy(source.at[window], target.at[window], sem.at[k, at])
+            copy.start()
+            copies.append(copy)
+    for copy in copies:
+        copy.wait()
+
+
+def prefetch(*arrays):
+    n = len(arrays)
+    size = sum(array.size * array.dtype.itemsize for array in arrays)
+    return pl.pallas_call(
+        prefetch_kernel,
+        in_specs=[pl.BlockSpec(memory_space=pl.ANY)] * n,
+        out_specs=[pl.BlockSpec(memory_space=pltpu.VMEM)] * n,
+        out_shape=[jax.ShapeDtypeStruct(array.shape, array.dtype) for array in arrays],
+        scratch_shapes=[pltpu.SemaphoreType.DMA((n, 4))],
+        compiler_params=pltpu.CompilerParams(vmem_limit_bytes=size + 2 * 1024 * 1024),
+        cost_estimate=pl.CostEstimate(flops=0, bytes_accessed=size, transcendentals=0),
+        name="prefetch",
+    )(*[pltpu.with_memory_space_constraint(array, pltpu.HBM) for array in arrays])
+
+
+def update_kernel(relatives, half, slabs, tile, *refs):
     n = len(relatives)
     rows_refs = refs[:n]
     signs_ref, weight_ref, second_ref = refs[n : n + 3]
-    new_weight_ref, new_second_ref, w_buf, s_buf, nw_buf, ns_buf, in_sem, out_sem = refs[-8:]
+    new_weight_ref, new_second_ref, nw_buf, ns_buf, out_sem = refs[-5:]
     part, low_rank = rows_refs[0].shape
     width = signs_ref.shape[0]
-    chunk = width // 2
-    inv_root = 1.0 / jnp.sqrt(jnp.full((1, 1), low_rank, jnp.float32))
+    slab = width // slabs
+    gain = math.sqrt(0.05) / math.sqrt(low_rank)
+    back = 0.5 / math.sqrt(0.05)
     nt = (((1,), (1,)), ((), ()))
-    tasks = []
-    for index, rel in enumerate(relatives):
-        first = pl.multiple_of(((place_ref[0] ^ rel) * 2 + half) * part, part)
-        for at in range(0, width, chunk):
-            slot = len(tasks)
-            window = (pl.ds(first, part), pl.ds(at, chunk))
-            loads = [
-                pltpu.make_async_copy(weight_ref.at[window], w_buf.at[slot], in_sem.at[0, slot]),
-                pltpu.make_async_copy(second_ref.at[window], s_buf.at[slot], in_sem.at[1, slot]),
-            ]
-            for load in loads:
-                load.start()
-            tasks.append((index, at, window, loads))
+    col = lax.axis_index("col")
+    firsts = [pl.multiple_of(((col ^ rel) * 2 + half) * part, part) for rel in relatives]
+    rows = jnp.concatenate([ref[...] for ref in rows_refs], axis=0) * gain
+    high = rows.astype(jnp.bfloat16)
+    low = (rows - high.astype(jnp.float32)).astype(jnp.bfloat16)
     stores = []
-    for slot, (index, at, window, loads) in enumerate(tasks):
-        rows = rows_refs[index][...]
-        high = rows.astype(jnp.bfloat16)
-        low = (rows - high.astype(jnp.float32)).astype(jnp.bfloat16)
-        signs = signs_ref[at : at + chunk, :]
-        dense_grad = lax.dot_general(high, signs, nt, preferred_element_type=jnp.float32)
-        dense_grad += lax.dot_general(low, signs, nt, preferred_element_type=jnp.float32)
-        dense_grad = dense_grad * inv_root
-        for load in loads:
-            load.wait()
-        new_second = 0.95 * s_buf[slot] + 0.05 * dense_grad * dense_grad
-        ns_buf[slot] = new_second
-        nw_buf[slot] = w_buf[slot] - 0.5 * dense_grad / (jnp.sqrt(new_second) + 1e-08)
-        for kind, (buf, ref) in enumerate(((nw_buf, new_weight_ref), (ns_buf, new_second_ref))):
-            store = pltpu.make_async_copy(buf.at[slot], ref.at[window], out_sem.at[kind, slot])
-            store.start()
-            stores.append(store)
+    for k in range(slabs):
+        for at in range(k * slab, (k + 1) * slab, tile):
+            signs = signs_ref[at : at + tile, :]
+            dense = lax.dot_general(high, signs, nt, preferred_element_type=jnp.float32)
+            dense += lax.dot_general(low, signs, nt, preferred_element_type=jnp.float32)
+            columns = slice(at - k * slab, at - k * slab + tile)
+            for b in range(n):
+                mine = dense[b * part : (b + 1) * part]
+                here = (pl.ds(firsts[b], part), slice(at, at + tile))
+                new_second = 0.95 * second_ref[here] + mine * mine
+                bottom = new_second * lax.rsqrt(new_second) + 1e-08
+                inverse = pl.reciprocal(bottom, approx=True)
+                inverse = inverse * (2.0 - bottom * inverse)
+                ns_buf[k * n + b, :, columns] = new_second
+                nw_buf[k * n + b, :, columns] = weight_ref[here] - (mine * back) * inverse
+        for b in range(n):
+            slot = k * n + b
+            window = (pl.ds(firsts[b], part), pl.ds(k * slab, slab))
+            for kind, (buf, ref) in enumerate(
+                ((nw_buf, new_weight_ref), (ns_buf, new_second_ref))
+            ):
+                store = pltpu.make_async_copy(
+                    buf.at[slot], ref.at[window], out_sem.at[kind, slot]
+                )
+                store.start()
+                stores.append(store)
     for store in stores:
         store.wait()
 
 
-def update(place, row_blocks, relatives, half, signs, weight, second, onto):
+def update(row_blocks, relatives, half, signs, weight, second, onto):
     part, low_rank = row_blocks[0].shape
     din_local = weight.shape[1]
     n = len(row_blocks)
-    slots, chunk = 2 * n, din_local // 2
+    slabs = 4
+    slab = din_local // slabs
     hbm = pl.BlockSpec(memory_space=pl.ANY)
     vmem = pl.BlockSpec(memory_space=pltpu.VMEM)
-    in_specs = [pl.BlockSpec(memory_space=pltpu.SMEM)] + [vmem] * (n + 1) + [hbm, hbm]
+    in_specs = [vmem] * (n + 3)
     aliases = {}
     if onto:
         in_specs += [hbm, hbm]
-        aliases = {n + 4: 0, n + 5: 1}
+        aliases = {n + 3: 0, n + 4: 1}
     size = n * part * din_local
-    buf = pltpu.VMEM((slots, part, chunk), jnp.float32)
+    buf = pltpu.VMEM((slabs * n, part, slab), jnp.float32)
     return pl.pallas_call(
-        functools.partial(update_kernel, relatives, half),
+        functools.partial(update_kernel, relatives, half, slabs, min(slab, 256)),
         in_specs=in_specs,
         out_specs=[hbm, hbm],
         out_shape=[
             jax.ShapeDtypeStruct(weight.shape, jnp.float32),
             jax.ShapeDtypeStruct(second.shape, jnp.float32),
         ],
-        scratch_shapes=[buf] * 4
-        + [pltpu.SemaphoreType.DMA((2, slots)), pltpu.SemaphoreType.DMA((2, slots))],
+        scratch_shapes=[buf, buf, pltpu.SemaphoreType.DMA((2, slabs * n))],
         input_output_aliases=aliases,
-        compiler_params=pltpu.CompilerParams(vmem_limit_bytes=24 * 1024 * 1024),
+        compiler_params=pltpu.CompilerParams(vmem_limit_bytes=12 * 1024 * 1024),
         cost_estimate=pl.CostEstimate(
-            flops=4 * size * low_rank, bytes_accessed=16 * size, transcendentals=2 * size
+            flops=4 * size * low_rank, bytes_accessed=8 * size, transcendentals=2 * size
         ),
         name="update",
-    )(
-        place,
-        *row_blocks,
-        signs,
-        pltpu.with_memory_space_constraint(weight, pltpu.HBM),
-        pltpu.with_memory_space_constraint(second, pltpu.HBM),
-        *onto,
-    )
+    )(*row_blocks, signs, weight, second, *onto)
 
 
 CORE, X, Y, Z0, Z1 = 1, 2, 4, 8, 16
@@ -377,12 +398,10 @@
     owner_rows = momentum.shape[0]
     total_tokens = lax.axis_size("dp") * tokens.shape[0]
     inv_root = 1.0 / jnp.sqrt(jnp.float32(low_rank))
-    place = jnp.stack(
-        [lax.axis_index("col").astype(jnp.int32), sign_seed[0], step_number[0]]
-    )
+    seeds = (sign_seed, step_number)
 
     far0 = [(Z1 | X | Z0, 0), (Z1 | X, 0), (Z1 | Z0, 0), (Z1, 0)]
-    near0 = [(Z0 | X, 0), (X, 0), (Z0, 0), (0, 0)]
+    near0 = [(Z0 | X, 0), (Z0, 0), (X, 0), (0, 0)]
     far1 = [(Z1 | Y | X, 1), (Z1 | Y, 1), (Z1 | X, 1), (Z1, 1)]
     near1 = [(Y | X, 1), (Y, 1), (X, 1), (0, 1)]
 
@@ -394,7 +413,7 @@
     og_y, og_z = pack(out_grad, [toward(Y, over_y), toward(Z0, over_z)], owner_rows, part)
     og_y = exchange(og_y, Y)
     og_z = exchange(og_z, Z0)
-    signs, send_a, keep_a = sketch_parts(place, tokens, low_rank, None)
+    signs, send_a, keep_a = sketch_parts(tokens, low_rank, None, seeds)
     og_yc, og_zc, og_c, og_own = pack(
         out_grad,
         [
@@ -411,7 +430,8 @@
     og_yc = exchange(og_yc, Y | CORE)
     og_zc = exchange(og_zc, Z0 | CORE)
     og_c = exchange(og_c, CORE)
-    send_b, keep_b = sketch_parts(place, tokens, low_rank, signs)
+    send_b, keep_b = sketch_parts(tokens, low_rank, signs, seeds)
+    weight_v, second_v = prefetch(weight, second)
     got_b = exchange(send_b, CORE)
     sketch = (((keep_b + got_b) + across) * inv_root).astype(jnp.bfloat16)
 
@@ -447,13 +467,13 @@
 
     far0_state = begin(y_side, (0, 0, 0, 0), X)
     far1_state = begin(z_side, (8, 8, 0, 0), Y)
-    near0_state = begin(y_side, (4, 4, 4, 4), X)
+    near0_state = begin(y_side, (4, 4, 4, 4), Z0)
     near1_state = begin(z_side, (12, 12, 4, 4), Y)
     far0_state = middle(far0_state, Z0)
     far1_state = middle(far1_state, X)
     last0 = exchange(packed(finish(far0_state), 2.0), Z1)
     last1 = exchange(packed(finish(far1_state), 2.0), Z1)
-    near0_state = middle(near0_state, Z0)
+    near0_state = middle(near0_state, X)
     near1_state = middle(near1_state, X)
 
     def momentum_half(half, near, last):
@@ -475,10 +495,10 @@
     done = ()
     for half in (0, 1):
         rows = (halves[half], pieces[half][0])
-        done = update(place, rows, (0, CORE), half, signs, weight, second, tuple(done))
+        done = update(rows, (0, CORE), half, signs, weight_v, second_v, tuple(done))
     for half in (0, 1):
         rows = (pieces[half][1], pieces[half][2])
-        done = update(place, rows, (X, X | CORE), half, signs, weight, second, tuple(done))
+        done = update(rows, (X, X | CORE), half, signs, weight_v, second_v, tuple(done))
     return (done[0], done[1], jnp.concatenate(halves, axis=0))
 
 

time: 136 us -> 123 us (0.904)
  Pallas kernels: 42.3 us -> 31.8 us
  local copies, waits for them, and re-layouts: 2.2 us -> 0.01 us
    pallas_call x6 -> x7, Pallas kernels: 35.2 us -> 24.9 us  [the longest x4 11.2 us: update(): pl.pallas_call(functools.partial(update_kernel, relatives, half, slabs, m...]
    unnamed x4 -> x2, local copies, waits for them, and re-layouts: 2.2 us -> 0.01 us
  transfers between devices with their start and end apart: 29 -> 29, of which waited for: 10 -> 11; matrix products, arithmetic and copies ran while one was open for 2% -> 2% of each run, Pallas kernels for 22% -> 19%
where the time goes in v1:
time: 123 us
  waiting for transfers between devices  55.8 us (45%)
  Pallas kernels  31.8 us (26%)
  starting transfers between devices  31.1 us (25%)
  between operations  2.37 us (2%)
  other arithmetic  2.05 us (2%)
    ppermute x29, waiting for transfers between devices, exchange(): return lax.ppermute(value, AXES, [(i, i ^ mask) for i in range(size)])  55.8 us
    ppermute x29, starting transfers between devices, exchange(): return lax.ppermute(value, AXES, [(i, i ^ mask) for i in range(size)])  31.1 us
    pallas_call x4, Pallas kernels, update(): pl.pallas_call(functools.partial(update_kernel, relatives, half, slabs, m...  11.2 us
    pallas_call x2, Pallas kernels, sketch_parts(): pl.pallas_call(functools.partial(sketch_kernel, first, din_local), in_spe...  7.8 us
    pallas_call x1, Pallas kernels, prefetch(): pl.pallas_call(prefetch_kernel, in_specs=[pl.BlockSpec(memory_space=pl.AN...  5.92 us
    pallas_call x2, Pallas kernels, pack(): pl.pallas_call(functools.partial(pack_kernel, groups, width, part), in_sp...  3.96 us
    pallas_call x4, Pallas kernels, project(): pl.pallas_call(functools.partial(project_kernel, n), grid=(1,), in_specs=...  2.92 us
  transfers between devices with their start and end apart: 29, of which 11 were waited for; matrix products, arithmetic and copies ran while one was open for 2% of the time, Pallas kernels for 19%

profile of v1, /device:TPU:0, one launch (start us, length us, event | category | flops | bytes accessed | tf_op | source)
XLA Modules:
  0.0 123.1 jit_solution(12510598261319325919)
XLA Ops:
  1.9 5.3 %sketch_first.1 = (bf16[2048,512]{1,0:T(8,128)(2,1)S(1)}, f32[256,512]{1,0:T(8,128)S(1)}, f32[256,512]{1,0:T(8,128)S(1)}) custom-call(s32[1]{0:T(128)S(6)} %copy.22.refs_0_, s32[1]{0:T(128)S(6)} %copy.23.refs_1_, bf16[1024,2048]{1,0:T(8,128)(2,1)} %refs_0_.3), custom_call_target="tpu_custom_call" | custom-call | flops 1073741824 | bytes 6291456 | tf_op jit(solution)/shard_map/sketch_first/pallas_call | solution.py:213
  7.2 0.6 collective-permute-start.1
  7.8 2.5 %sketch_next.1 = (f32[256,512]{1,0:T(8,128)S(1)}, f32[256,512]{1,0:T(8,128)S(1)}) custom-call(bf16[1024,2048]{1,0:T(8,128)(2,1)} %refs_0_.3, bf16[2048,512]{1,0:T(8,128)(2,1)S(1)} %get-tuple-element.33.refs_1_.refs_2_), custom_call_target="tpu_custom_call" | custom-call | flops 1073741824 | bytes 6291456 | tf_op jit(solution)/shard_map/sketch_next/pallas_call | solution.py:213
  10.5 3.0 %collective-permute-start.2 = (f32[256,512]{1,0:T(8,128)S(1)}, f32[256,512]{1,0:T(8,128)S(1)}, u32[]{:S(2)}, u32[]{:S(2)}) collective-permute-start(f32[256,512]{1,0:T(8,128)S(1)} %add.74), channel_id=1, source_target_pairs={{0,2},{1,3},{2,0},{3,1},{4,6},{5,7},{6,4},{7,5},{8,10},{9,11},{10,... | collective-permute-start | bytes 1572872 | tf_op jit(solution)/shard_map/ppermute | solution.py:393
  13.5 2.5 %pack.2 = (bf16[8,256,128]{2,1,0:T(8,128)(2,1)S(1)}, bf16[8,256,128]{2,1,0:T(8,128)(2,1)S(1)}, bf16[16,256,128]{2,1,0:T(8,128)(2,1)S(1)}, bf16[16,256,128]{2,1,0:T(8,128)(2,1)S(1)}) custom-call(bf16[256,8192]{1,0:T(8,128)(2,1)} %og_ref.3), custom_call_target="tpu_custom_call" | custom-call | bytes 6291456 | tf_op jit(solution)/shard_map/pack/pallas_call | solution.py:126
  16.1 1.6 %collective-permute-start.17 = (bf16[8,256,128]{2,1,0:T(8,128)(2,1)S(1)}, bf16[8,256,128]{2,1,0:T(8,128)(2,1)S(1)}, u32[]{:S(2)}, u32[]{:S(2)}) collective-permute-start(bf16[8,256,128]{2,1,0:T(8,128)(2,1)S(1)} %get-tuple-element.47), channel_id=1, source_target_pairs={{0,5},{1,4},{2,7},{3,6},{4,1},{5,0},{6,3},{7,2},{8,13},{9,12},{10,... | collective-permute-start | bytes 1572872 | tf_op jit(solution)/shard_map/ppermute | solution.py:393
  17.7 1.5 %pack.3 = (bf16[8,256,128]{2,1,0:T(8,128)(2,1)S(1)}, bf16[8,256,128]{2,1,0:T(8,128)(2,1)S(1)}) custom-call(bf16[256,8192]{1,0:T(8,128)(2,1)} %og_ref.3), custom_call_target="tpu_custom_call" | custom-call | bytes 2097152 | tf_op jit(solution)/shard_map/pack/pallas_call | solution.py:126
  19.2 0.6 collective-permute-start.16
  19.8 5.9 %collective-permute-done.2 = f32[256,512]{1,0:T(8,128)S(1)} collective-permute-done((f32[256,512]{1,0:T(8,128)S(1)}, f32[256,512]{1,0:T(8,128)S(1)}, u32[]{:S(2)}, u32[]{:S(2)}) %collective-permute-start.2) | collective-permute-done | bytes 524320 | tf_op jit(solution)/shard_map/ppermute | solution.py:393
  25.8 1.8 %collective-permute-start.14 = (bf16[256,512]{1,0:T(8,128)(2,1)S(1)}, bf16[256,512]{1,0:T(8,128)(2,1)S(1)}, u32[]{:S(2)}, u32[]{:S(2)}) collective-permute-start(bf16[256,512]{1,0:T(8,128)(2,1)S(1)} %multiply_convert_fusion.4.refs_0_), channel_id=1, source_target_pairs={{0,4},{1,5},{2,6},{3,7},{4,0},{5,1},{6,2},{7,3},{8,12},{9,13},{10,... | collective-permute-start | bytes 786440 | tf_op jit(solution)/shard_map/ppermute | solution.py:393
  27.6 1.6 %collective-permute-start.4 = (bf16[256,512]{1,0:T(8,128)(2,1)S(1)}, bf16[256,512]{1,0:T(8,128)(2,1)S(1)}, u32[]{:S(2)}, u32[]{:S(2)}) collective-permute-start(bf16[256,512]{1,0:T(8,128)(2,1)S(1)} %multiply_convert_fusion.4.refs_0_), channel_id=1, source_target_pairs={{0,8},{1,9},{2,10},{3,11},{4,12},{5,13},{6,14},{7,15},{8,0},{9,1},... | collective-permute-start | bytes 786440 | tf_op jit(solution)/shard_map/ppermute | solution.py:393
  29.2 0.8 collective-permute-done.17.refs_7_
  30.0 0.8 collective-permute-start.3
  30.8 16.4 %collective-permute-done.14.refs_2_ = bf16[256,512]{1,0:T(8,128)(2,1)S(1)} collective-permute-done((bf16[256,512]{1,0:T(8,128)(2,1)S(1)}, bf16[256,512]{1,0:T(8,128)(2,1)S(1)}, u32[]{:S(2)}, u32[]{:S(2)}) %collective-permute-start.14) | collective-permute-done | bytes 262176 | tf_op jit(solution)/shard_map/ppermute | solution.py:393
  47.2 5.9 %prefetch.1 = (f32[1024,2048]{1,0:T(8,128)S(1)}, f32[1024,2048]{1,0:T(8,128)S(1)}) custom-call(f32[1024,2048]{1,0:T(8,128)} %refs_0_.4, f32[1024,2048]{1,0:T(8,128)} %refs_1_.2), custom_call_target="tpu_custom_call" | custom-call | bytes 16777216 | tf_op jit(solution)/shard_map/prefetch/pallas_call | solution.py:296
  53.2 1.7 %collective-permute-start.8 = (bf16[8,256,128]{2,1,0:T(8,128)(2,1)S(1)}, bf16[8,256,128]{2,1,0:T(8,128)(2,1)S(1)}, u32[]{:S(2)}, u32[]{:S(2)}) collective-permute-start(bf16[8,256,128]{2,1,0:T(8,128)(2,1)S(1)} %get-tuple-element.41), channel_id=1, source_target_pairs={{0,9},{1,8},{2,11},{3,10},{4,13},{5,12},{6,15},{7,14},{8,1},{9,0},... | collective-permute-start | bytes 1572872 | tf_op jit(solution)/shard_map/ppermute | solution.py:393
  54.9 0.5 collective-permute-start.7
  55.4 0.7 project.6
  56.2 1.6 %collective-permute-start.18 = (f16[2,128,512]{2,1,0:T(8,128)(2,1)S(1)}, f16[2,128,512]{2,1,0:T(8,128)(2,1)S(1)}, u32[]{:S(2)}, u32[]{:S(2)}) collective-permute-start(f16[2,128,512]{2,1,0:T(8,128)(2,1)S(1)} %multiply_convert_fusion.1), channel_id=1, source_target_pairs={{0,8},{1,9},{2,10},{3,11},{4,12},{5,13},{6,14},{7,15},{8,0},{9,1},... | collective-permute-start | bytes 786440 | tf_op jit(solution)/shard_map/ppermute | solution.py:393
  57.9 0.7 project.7
  58.6 0.6 collective-permute-start.20
  59.2 8.0 %collective-permute-done.8.refs_7_ = bf16[8,256,128]{2,1,0:T(8,128)(2,1)S(1)} collective-permute-done((bf16[8,256,128]{2,1,0:T(8,128)(2,1)S(1)}, bf16[8,256,128]{2,1,0:T(8,128)(2,1)S(1)}, u32[]{:S(2)}, u32[]{:S(2)}) %collective-permute-start.8) | collective-permute-done | bytes 524320 | tf_op jit(solution)/shard_map/ppermute | solution.py:393
  67.3 12.1 %collective-permute-done.7.refs_6_ = bf16[8,256,128]{2,1,0:T(8,128)(2,1)S(1)} collective-permute-done((bf16[8,256,128]{2,1,0:T(8,128)(2,1)S(1)}, bf16[8,256,128]{2,1,0:T(8,128)(2,1)S(1)}, u32[]{:S(2)}, u32[]{:S(2)}) %collective-permute-start.7) | collective-permute-done | bytes 524320 | tf_op jit(solution)/shard_map/ppermute | solution.py:393
  79.4 0.7 project.4
  80.2 1.6 %collective-permute-start.9 = (f16[2,128,512]{2,1,0:T(8,128)(2,1)S(1)}, f16[2,128,512]{2,1,0:T(8,128)(2,1)S(1)}, u32[]{:S(2)}, u32[]{:S(2)}) collective-permute-start(f16[2,128,512]{2,1,0:T(8,128)(2,1)S(1)} %multiply_convert_fusion.3), channel_id=1, source_target_pairs={{0,4},{1,5},{2,6},{3,7},{4,0},{5,1},{6,2},{7,3},{8,12},{9,13},{10,... | collective-permute-start | bytes 786440 | tf_op jit(solution)/shard_map/ppermute | solution.py:393
  81.8 0.7 project.5
  82.6 0.6 collective-permute-start.11
  83.1 1.2 collective-permute-done.18
  84.4 0.5 collective-permute-start.19
  85.0 1.7 %collective-permute-start.21 = (f16[128,512]{1,0:T(8,128)(2,1)S(1)}, f16[128,512]{1,0:T(8,128)(2,1)S(1)}, u32[]{:S(2)}, u32[]{:S(2)}) collective-permute-start(f16[128,512]{1,0:T(8,128)(2,1)S(1)} %fusion.13), channel_id=1, source_target_pairs={{0,8},{1,9},{2,10},{3,11},{4,12},{5,13},{6,14},{7,15},{8,0},{9,1},... | collective-permute-start | bytes 393224 | tf_op jit(solution)/shard_map/ppermute | solution.py:393
  86.7 2.8 %collective-permute-done.9 = f16[2,128,512]{2,1,0:T(8,128)(2,1)S(1)} collective-permute-done((f16[2,128,512]{2,1,0:T(8,128)(2,1)S(1)}, f16[2,128,512]{2,1,0:T(8,128)(2,1)S(1)}, u32[]{:S(2)}, u32[]{:S(2)}) %collective-permute-start.9) | collective-permute-done | bytes 262176 | tf_op jit(solution)/shard_map/ppermute | solution.py:393
  89.5 0.4 collective-permute-start.10
  89.9 2.9 %collective-permute-done.11 = f16[2,128,512]{2,1,0:T(8,128)(2,1)S(1)} collective-permute-done((f16[2,128,512]{2,1,0:T(8,128)(2,1)S(1)}, f16[2,128,512]{2,1,0:T(8,128)(2,1)S(1)}, u32[]{:S(2)}, u32[]{:S(2)}) %collective-permute-start.11) | collective-permute-done | bytes 262176 | tf_op jit(solution)/shard_map/ppermute | solution.py:393
  92.9 0.7 collective-permute-start.12
  93.6 2.6 %collective-permute-start.22 = (f16[128,512]{1,0:T(8,128)(2,1)S(1)}, f16[128,512]{1,0:T(8,128)(2,1)S(1)}, u32[]{:S(2)}, u32[]{:S(2)}) collective-permute-start(f16[128,512]{1,0:T(8,128)(2,1)S(1)} %fusion.1), channel_id=1, source_target_pairs={{0,16},{1,17},{2,18},{3,19},{4,20},{5,21},{6,22},{7,23},{8,24},{9,... | collective-permute-start | bytes 393224 | tf_op jit(solution)/shard_map/ppermute | solution.py:393
  96.2 1.7 %collective-permute-done.12 = f16[128,512]{1,0:T(8,128)(2,1)S(1)} collective-permute-done((f16[128,512]{1,0:T(8,128)(2,1)S(1)}, f16[128,512]{1,0:T(8,128)(2,1)S(1)}, u32[]{:S(2)}, u32[]{:S(2)}) %collective-permute-start.12) | collective-permute-done | bytes 131104 | tf_op jit(solution)/shard_map/ppermute | solution.py:393
  98.0 2.6 %collective-permute-start.13 = (f16[128,512]{1,0:T(8,128)(2,1)S(1)}, f16[128,512]{1,0:T(8,128)(2,1)S(1)}, u32[]{:S(2)}, u32[]{:S(2)}) collective-permute-start(f16[128,512]{1,0:T(8,128)(2,1)S(1)} %fusion.6), channel_id=1, source_target_pairs={{0,16},{1,17},{2,18},{3,19},{4,20},{5,21},{6,22},{7,23},{8,24},{9,... | collective-permute-start | bytes 393224 | tf_op jit(solution)/shard_map/ppermute | solution.py:393
  100.7 2.1 %collective-permute-done.22 = f16[128,512]{1,0:T(8,128)(2,1)S(1)} collective-permute-done((f16[128,512]{1,0:T(8,128)(2,1)S(1)}, f16[128,512]{1,0:T(8,128)(2,1)S(1)}, u32[]{:S(2)}, u32[]{:S(2)}) %collective-permute-start.22) | collective-permute-done | bytes 131104 | tf_op jit(solution)/shard_map/ppermute | solution.py:393
  103.0 3.7 %collective-permute-start.25 = (f16[128,512]{1,0:T(8,128)(2,1)S(1)}, f16[128,512]{1,0:T(8,128)(2,1)S(1)}, u32[]{:S(2)}, u32[]{:S(2)}) collective-permute-start(f16[128,512]{1,0:T(8,128)(2,1)S(1)} %get-tuple-element.65), channel_id=1, source_target_pairs={{0,2},{1,3},{2,0},{3,1},{4,6},{5,7},{6,4},{7,5},{8,10},{9,11},{10,... | collective-permute-start | bytes 393224 | tf_op jit(solution)/shard_map/ppermute | solution.py:393
  106.8 0.2 collective-permute-start.27
  107.0 1.3 %collective-permute-start.23 = (f16[128,512]{1,0:T(8,128)(2,1)S(1)}, f16[128,512]{1,0:T(8,128)(2,1)S(1)}, u32[]{:S(2)}, u32[]{:S(2)}) collective-permute-start(f16[128,512]{1,0:T(8,128)(2,1)S(1)} %get-tuple-element.63), channel_id=1, source_target_pairs={{0,2},{1,3},{2,0},{3,1},{4,6},{5,7},{6,4},{7,5},{8,10},{9,11},{10,... | collective-permute-start | bytes 393224 | tf_op jit(solution)/shard_map/ppermute | solution.py:393
  108.3 0.8 pad_maximum_fusion
  109.2 1.8 %collective-permute-done.25 = f16[128,512]{1,0:T(8,128)(2,1)S(1)} collective-permute-done((f16[128,512]{1,0:T(8,128)(2,1)S(1)}, f16[128,512]{1,0:T(8,128)(2,1)S(1)}, u32[]{:S(2)}, u32[]{:S(2)}) %collective-permute-start.25) | collective-permute-done | bytes 131104 | tf_op jit(solution)/shard_map/ppermute | solution.py:393
  111.0 2.8 %update.4 = (f32[1024,2048]{1,0:T(8,128)}, f32[1024,2048]{1,0:T(8,128)}) custom-call(f32[128,512]{1,0:T(8,128)S(1)} %get-tuple-element.66.refs_0_, f32[128,512]{1,0:T(8,128)S(1)} %convert_element_type.127.refs_1_, bf16[2048,512]{1,0:T(8,128)(2,1)S(1)} %get-tuple-element.33.refs_1_.refs_2_, f32[1024,2048]{1,0:T(8,128)S(1)} %get-tuple-element.53.refs_3_, ...), custom_call_target="tpu_custom_call" | custom-call | flops 1073741824 | bytes 4194304 | tf_op jit(solution)/shard_map/update/pallas_call | solution.py:370
  113.8 0.6 collective-permute-start.24
  114.4 2.8 %update.5 = (f32[1024,2048]{1,0:T(8,128)}, f32[1024,2048]{1,0:T(8,128)}) custom-call(f32[128,512]{1,0:T(8,128)S(1)} %get-tuple-element.64.refs_0_, f32[128,512]{1,0:T(8,128)S(1)} %convert_element_type.126.refs_1_, bf16[2048,512]{1,0:T(8,128)(2,1)S(1)} %get-tuple-element.33.refs_1_.refs_2_, ...), custom_call_target="tpu_custom_call", output_to_operand_aliasing={{0}: (5, {}), {1}: (6, {})} | custom-call | flops 1073741824 | bytes 4194304 | tf_op jit(solution)/shard_map/update/pallas_call | solution.py:370
  117.3 2.8 %update.6 = (f32[1024,2048]{1,0:T(8,128)}, f32[1024,2048]{1,0:T(8,128)}) custom-call(f32[128,512]{1,0:T(8,128)S(1)} %convert_element_type.124.refs_0_, f32[128,512]{1,0:T(8,128)S(1)} %convert_element_type.125.refs_1_, bf16[2048,512]{1,0:T(8,128)(2,1)S(1)} %get-tuple-element.33.refs_1_.refs_2_, ...), custom_call_target="tpu_custom_call", output_to_operand_aliasing={{0}: (5, {}), {1}: (6, {})} | custom-call | flops 1073741824 | bytes 4194304 | tf_op jit(solution)/shard_map/update/pallas_call | solution.py:370
  120.2 2.8 %update.7 = (f32[1024,2048]{1,0:T(8,128)}, f32[1024,2048]{1,0:T(8,128)}) custom-call(f32[128,512]{1,0:T(8,128)S(1)} %convert_element_type.122.refs_0_, f32[128,512]{1,0:T(8,128)S(1)} %convert_element_type.123.refs_1_, bf16[2048,512]{1,0:T(8,128)(2,1)S(1)} %get-tuple-element.33.refs_1_.refs_2_, ...), custom_call_target="tpu_custom_call", output_to_operand_aliasing={{0}: (5, {}), {1}: (6, {})} | custom-call | flops 1073741824 | bytes 4194304 | tf_op jit(solution)/shard_map/update/pallas_call | solution.py:370
  (46 shorter events, 1.5 us)
Async XLA Ops:
  7.2 3.2 %collective-permute-start.1 = (f32[256,512]{1,0:T(8,128)S(1)}, f32[256,512]{1,0:T(8,128)S(1)}, u32[]{:S(2)}, u32[]{:S(2)}) collective-permute-start(f32[256,512]{1,0:T(8,128)S(1)} %get-tuple-element.37), channel_id=1, source_target_pairs={{0,1},{1,0},{2,3},{3,2},{4,5},{5,4},{6,7},{7,6},{8,9},{9,8},{10,11... | collective-permute-start | bytes 1572872 | tf_op jit(solution)/shard_map/ppermute | solution.py:393
  10.3 9.5 %collective-permute-start = (f32[256,512]{1,0:T(8,128)S(1)}, f32[256,512]{1,0:T(8,128)S(1)}, u32[]{:S(2)}, u32[]{:S(2)}) collective-permute-start(f32[256,512]{1,0:T(8,128)S(1)} %get-tuple-element.35), channel_id=1, source_target_pairs={{0,1},{1,0},{2,3},{3,2},{4,5},{5,4},{6,7},{7,6},{8,9},{9,8},{10,11... | collective-permute-start | bytes 1572872 | tf_op jit(solution)/shard_map/ppermute | solution.py:393
  10.5 15.2 %collective-permute-start.2 = (f32[256,512]{1,0:T(8,128)S(1)}, f32[256,512]{1,0:T(8,128)S(1)}, u32[]{:S(2)}, u32[]{:S(2)}) collective-permute-start(f32[256,512]{1,0:T(8,128)S(1)} %add.74), channel_id=1, source_target_pairs={{0,2},{1,3},{2,0},{3,1},{4,6},{5,7},{6,4},{7,5},{8,10},{9,11},{10,... | collective-permute-start | bytes 1572872 | tf_op jit(solution)/shard_map/ppermute | solution.py:393
  16.0 38.9 %collective-permute-start.6 = (bf16[16,256,128]{2,1,0:T(8,128)(2,1)S(1)}, bf16[16,256,128]{2,1,0:T(8,128)(2,1)S(1)}, u32[]{:S(2)}, u32[]{:S(2)}) collective-permute-start(bf16[16,256,128]{2,1,0:T(8,128)(2,1)S(1)} %get-tuple-element.39), channel_id=1, source_target_pairs={{0,1},{1,0},{2,3},{3,2},{4,5},{5,4},{6,7},{7,6},{8,9},{9,8},{10,11... | collective-permute-start | bytes 3145736 | tf_op jit(solution)/shard_map/ppermute | solution.py:393
  16.1 13.9 %collective-permute-start.17 = (bf16[8,256,128]{2,1,0:T(8,128)(2,1)S(1)}, bf16[8,256,128]{2,1,0:T(8,128)(2,1)S(1)}, u32[]{:S(2)}, u32[]{:S(2)}) collective-permute-start(bf16[8,256,128]{2,1,0:T(8,128)(2,1)S(1)} %get-tuple-element.47), channel_id=1, source_target_pairs={{0,5},{1,4},{2,7},{3,6},{4,1},{5,0},{6,3},{7,2},{8,13},{9,12},{10,... | collective-permute-start | bytes 1572872 | tf_op jit(solution)/shard_map/ppermute | solution.py:393
  19.2 34.0 %collective-permute-start.16 = (bf16[8,256,128]{2,1,0:T(8,128)(2,1)S(1)}, bf16[8,256,128]{2,1,0:T(8,128)(2,1)S(1)}, u32[]{:S(2)}, u32[]{:S(2)}) collective-permute-start(bf16[8,256,128]{2,1,0:T(8,128)(2,1)S(1)} %get-tuple-element.46), channel_id=1, source_target_pairs={{0,4},{1,5},{2,6},{3,7},{4,0},{5,1},{6,2},{7,3},{8,12},{9,13},{10,... | collective-permute-start | bytes 1572872 | tf_op jit(solution)/shard_map/ppermute | solution.py:393
  25.8 21.4 %collective-permute-start.14 = (bf16[256,512]{1,0:T(8,128)(2,1)S(1)}, bf16[256,512]{1,0:T(8,128)(2,1)S(1)}, u32[]{:S(2)}, u32[]{:S(2)}) collective-permute-start(bf16[256,512]{1,0:T(8,128)(2,1)S(1)} %multiply_convert_fusion.4.refs_0_), channel_id=1, source_target_pairs={{0,4},{1,5},{2,6},{3,7},{4,0},{5,1},{6,2},{7,3},{8,12},{9,13},{10,... | collective-permute-start | bytes 786440 | tf_op jit(solution)/shard_map/ppermute | solution.py:393
  27.6 27.8 %collective-permute-start.4 = (bf16[256,512]{1,0:T(8,128)(2,1)S(1)}, bf16[256,512]{1,0:T(8,128)(2,1)S(1)}, u32[]{:S(2)}, u32[]{:S(2)}) collective-permute-start(bf16[256,512]{1,0:T(8,128)(2,1)S(1)} %multiply_convert_fusion.4.refs_0_), channel_id=1, source_target_pairs={{0,8},{1,9},{2,10},{3,11},{4,12},{5,13},{6,14},{7,15},{8,0},{9,1},... | collective-permute-start | bytes 786440 | tf_op jit(solution)/shard_map/ppermute | solution.py:393
  30.0 25.4 %collective-permute-start.3 = (bf16[256,512]{1,0:T(8,128)(2,1)S(1)}, bf16[256,512]{1,0:T(8,128)(2,1)S(1)}, u32[]{:S(2)}, u32[]{:S(2)}) collective-permute-start(bf16[256,512]{1,0:T(8,128)(2,1)S(1)} %multiply_convert_fusion.4.refs_0_), channel_id=1, source_target_pairs={{0,1},{1,0},{2,3},{3,2},{4,5},{5,4},{6,7},{7,6},{8,9},{9,8},{10,11... | collective-permute-start | bytes 786440 | tf_op jit(solution)/shard_map/ppermute | solution.py:393
  47.2 8.2 %collective-permute-start.15 = (bf16[256,512]{1,0:T(8,128)(2,1)S(1)}, bf16[256,512]{1,0:T(8,128)(2,1)S(1)}, u32[]{:S(2)}, u32[]{:S(2)}) collective-permute-start(bf16[256,512]{1,0:T(8,128)(2,1)S(1)} %collective-permute-done.14.refs_2_), channel_id=1, source_target_pairs={{0,1},{1,0},{2,3},{3,2},{4,5},{5,4},{6,7},{7,6},{8,9},{9,8},{10,11... | collective-permute-start | bytes 786440 | tf_op jit(solution)/shard_map/ppermute | solution.py:393
  53.2 14.1 %collective-permute-start.8 = (bf16[8,256,128]{2,1,0:T(8,128)(2,1)S(1)}, bf16[8,256,128]{2,1,0:T(8,128)(2,1)S(1)}, u32[]{:S(2)}, u32[]{:S(2)}) collective-permute-start(bf16[8,256,128]{2,1,0:T(8,128)(2,1)S(1)} %get-tuple-element.41), channel_id=1, source_target_pairs={{0,9},{1,8},{2,11},{3,10},{4,13},{5,12},{6,15},{7,14},{8,1},{9,0},... | collective-permute-start | bytes 1572872 | tf_op jit(solution)/shard_map/ppermute | solution.py:393
  54.9 24.5 %collective-permute-start.7 = (bf16[8,256,128]{2,1,0:T(8,128)(2,1)S(1)}, bf16[8,256,128]{2,1,0:T(8,128)(2,1)S(1)}, u32[]{:S(2)}, u32[]{:S(2)}) collective-permute-start(bf16[8,256,128]{2,1,0:T(8,128)(2,1)S(1)} %get-tuple-element.40), channel_id=1, source_target_pairs={{0,8},{1,9},{2,10},{3,11},{4,12},{5,13},{6,14},{7,15},{8,0},{9,1},... | collective-permute-start | bytes 1572872 | tf_op jit(solution)/shard_map/ppermute | solution.py:393
  55.4 24.0 %collective-permute-start.5 = (bf16[256,512]{1,0:T(8,128)(2,1)S(1)}, bf16[256,512]{1,0:T(8,128)(2,1)S(1)}, u32[]{:S(2)}, u32[]{:S(2)}) collective-permute-start(bf16[256,512]{1,0:T(8,128)(2,1)S(1)} %collective-permute-done.4.refs_2_), channel_id=1, source_target_pairs={{0,1},{1,0},{2,3},{3,2},{4,5},{5,4},{6,7},{7,6},{8,9},{9,8},{10,11... | collective-permute-start | bytes 786440 | tf_op jit(solution)/shard_map/ppermute | solution.py:393
  56.2 46.5 %copy-start = (f32[256,512]{1,0:T(8,128)S(1)}, f32[256,512]{1,0:T(8,128)}, u32[]{:S(2)}) copy-start(f32[256,512]{1,0:T(8,128)} %param.11) | copy-start | bytes 1572868
  56.2 28.1 %collective-permute-start.18 = (f16[2,128,512]{2,1,0:T(8,128)(2,1)S(1)}, f16[2,128,512]{2,1,0:T(8,128)(2,1)S(1)}, u32[]{:S(2)}, u32[]{:S(2)}) collective-permute-start(f16[2,128,512]{2,1,0:T(8,128)(2,1)S(1)} %multiply_convert_fusion.1), channel_id=1, source_target_pairs={{0,8},{1,9},{2,10},{3,11},{4,12},{5,13},{6,14},{7,15},{8,0},{9,1},... | collective-permute-start | bytes 786440 | tf_op jit(solution)/shard_map/ppermute | solution.py:393
  58.6 26.3 %collective-permute-start.20 = (f16[2,128,512]{2,1,0:T(8,128)(2,1)S(1)}, f16[2,128,512]{2,1,0:T(8,128)(2,1)S(1)}, u32[]{:S(2)}, u32[]{:S(2)}) collective-permute-start(f16[2,128,512]{2,1,0:T(8,128)(2,1)S(1)} %multiply_convert_fusion), channel_id=1, source_target_pairs={{0,2},{1,3},{2,0},{3,1},{4,6},{5,7},{6,4},{7,5},{8,10},{9,11},{10,... | collective-permute-start | bytes 786440 | tf_op jit(solution)/shard_map/ppermute | solution.py:393
  80.2 9.2 %collective-permute-start.9 = (f16[2,128,512]{2,1,0:T(8,128)(2,1)S(1)}, f16[2,128,512]{2,1,0:T(8,128)(2,1)S(1)}, u32[]{:S(2)}, u32[]{:S(2)}) collective-permute-start(f16[2,128,512]{2,1,0:T(8,128)(2,1)S(1)} %multiply_convert_fusion.3), channel_id=1, source_target_pairs={{0,4},{1,5},{2,6},{3,7},{4,0},{5,1},{6,2},{7,3},{8,12},{9,13},{10,... | collective-permute-start | bytes 786440 | tf_op jit(solution)/shard_map/ppermute | solution.py:393
  82.6 10.3 %collective-permute-start.11 = (f16[2,128,512]{2,1,0:T(8,128)(2,1)S(1)}, f16[2,128,512]{2,1,0:T(8,128)(2,1)S(1)}, u32[]{:S(2)}, u32[]{:S(2)}) collective-permute-start(f16[2,128,512]{2,1,0:T(8,128)(2,1)S(1)} %multiply_convert_fusion.2), channel_id=1, source_target_pairs={{0,4},{1,5},{2,6},{3,7},{4,0},{5,1},{6,2},{7,3},{8,12},{9,13},{10,... | collective-permute-start | bytes 786440 | tf_op jit(solution)/shard_map/ppermute | solution.py:393
  84.4 16.3 %collective-permute-start.19 = (f16[128,512]{1,0:T(8,128)(2,1)S(1)}, f16[128,512]{1,0:T(8,128)(2,1)S(1)}, u32[]{:S(2)}, u32[]{:S(2)}) collective-permute-start(f16[128,512]{1,0:T(8,128)(2,1)S(1)} %fusion.12), channel_id=1, source_target_pairs={{0,2},{1,3},{2,0},{3,1},{4,6},{5,7},{6,4},{7,5},{8,10},{9,11},{10,... | collective-permute-start | bytes 393224 | tf_op jit(solution)/shard_map/ppermute | solution.py:393
  85.0 8.6 %collective-permute-start.21 = (f16[128,512]{1,0:T(8,128)(2,1)S(1)}, f16[128,512]{1,0:T(8,128)(2,1)S(1)}, u32[]{:S(2)}, u32[]{:S(2)}) collective-permute-start(f16[128,512]{1,0:T(8,128)(2,1)S(1)} %fusion.13), channel_id=1, source_target_pairs={{0,8},{1,9},{2,10},{3,11},{4,12},{5,13},{6,14},{7,15},{8,0},{9,1},... | collective-permute-start | bytes 393224 | tf_op jit(solution)/shard_map/ppermute | solution.py:393
  89.5 17.1 %collective-permute-start.10 = (f16[128,512]{1,0:T(8,128)(2,1)S(1)}, f16[128,512]{1,0:T(8,128)(2,1)S(1)}, u32[]{:S(2)}, u32[]{:S(2)}) collective-permute-start(f16[128,512]{1,0:T(8,128)(2,1)S(1)} %fusion.10), channel_id=1, source_target_pairs={{0,2},{1,3},{2,0},{3,1},{4,6},{5,7},{6,4},{7,5},{8,10},{9,11},{10,... | collective-permute-start | bytes 393224 | tf_op jit(solution)/shard_map/ppermute | solution.py:393
  92.9 5.0 %collective-permute-start.12 = (f16[128,512]{1,0:T(8,128)(2,1)S(1)}, f16[128,512]{1,0:T(8,128)(2,1)S(1)}, u32[]{:S(2)}, u32[]{:S(2)}) collective-permute-start(f16[128,512]{1,0:T(8,128)(2,1)S(1)} %fusion.11), channel_id=1, source_target_pairs={{0,2},{1,3},{2,0},{3,1},{4,6},{5,7},{6,4},{7,5},{8,10},{9,11},{10,... | collective-permute-start | bytes 393224 | tf_op jit(solution)/shard_map/ppermute | solution.py:393
  93.6 9.1 %collective-permute-start.22 = (f16[128,512]{1,0:T(8,128)(2,1)S(1)}, f16[128,512]{1,0:T(8,128)(2,1)S(1)}, u32[]{:S(2)}, u32[]{:S(2)}) collective-permute-start(f16[128,512]{1,0:T(8,128)(2,1)S(1)} %fusion.1), channel_id=1, source_target_pairs={{0,16},{1,17},{2,18},{3,19},{4,20},{5,21},{6,22},{7,23},{8,24},{9,... | collective-permute-start | bytes 393224 | tf_op jit(solution)/shard_map/ppermute | solution.py:393
  98.0 8.6 %collective-permute-start.13 = (f16[128,512]{1,0:T(8,128)(2,1)S(1)}, f16[128,512]{1,0:T(8,128)(2,1)S(1)}, u32[]{:S(2)}, u32[]{:S(2)}) collective-permute-start(f16[128,512]{1,0:T(8,128)(2,1)S(1)} %fusion.6), channel_id=1, source_target_pairs={{0,16},{1,17},{2,18},{3,19},{4,20},{5,21},{6,22},{7,23},{8,24},{9,... | collective-permute-start | bytes 393224 | tf_op jit(solution)/shard_map/ppermute | solution.py:393
  102.9 6.3 %collective-permute-start.28 = (f16[128,512]{1,0:T(8,128)(2,1)S(1)}, f16[128,512]{1,0:T(8,128)(2,1)S(1)}, u32[]{:S(2)}, u32[]{:S(2)}) collective-permute-start(f16[128,512]{1,0:T(8,128)(2,1)S(1)} %get-tuple-element.65), channel_id=1, source_target_pairs={{0,1},{1,0},{2,3},{3,2},{4,5},{5,4},{6,7},{7,6},{8,9},{9,8},{10,11... | collective-permute-start | bytes 393224 | tf_op jit(solution)/shard_map/ppermute | solution.py:393
  103.0 8.0 %collective-permute-start.25 = (f16[128,512]{1,0:T(8,128)(2,1)S(1)}, f16[128,512]{1,0:T(8,128)(2,1)S(1)}, u32[]{:S(2)}, u32[]{:S(2)}) collective-permute-start(f16[128,512]{1,0:T(8,128)(2,1)S(1)} %get-tuple-element.65), channel_id=1, source_target_pairs={{0,2},{1,3},{2,0},{3,1},{4,6},{5,7},{6,4},{7,5},{8,10},{9,11},{10,... | collective-permute-start | bytes 393224 | tf_op jit(solution)/shard_map/ppermute | solution.py:393
  106.8 7.0 %collective-permute-start.27 = (f16[128,512]{1,0:T(8,128)(2,1)S(1)}, f16[128,512]{1,0:T(8,128)(2,1)S(1)}, u32[]{:S(2)}, u32[]{:S(2)}) collective-permute-start(f16[128,512]{1,0:T(8,128)(2,1)S(1)} %get-tuple-element.63), channel_id=1, source_target_pairs={{0,1},{1,0},{2,3},{3,2},{4,5},{5,4},{6,7},{7,6},{8,9},{9,8},{10,11... | collective-permute-start | bytes 393224 | tf_op jit(solution)/shard_map/ppermute | solution.py:393
  107.0 6.8 %collective-permute-start.23 = (f16[128,512]{1,0:T(8,128)(2,1)S(1)}, f16[128,512]{1,0:T(8,128)(2,1)S(1)}, u32[]{:S(2)}, u32[]{:S(2)}) collective-permute-start(f16[128,512]{1,0:T(8,128)(2,1)S(1)} %get-tuple-element.63), channel_id=1, source_target_pairs={{0,2},{1,3},{2,0},{3,1},{4,6},{5,7},{6,4},{7,5},{8,10},{9,11},{10,... | collective-permute-start | bytes 393224 | tf_op jit(solution)/shard_map/ppermute | solution.py:393
  111.0 6.3 %collective-permute-start.26 = (f16[128,512]{1,0:T(8,128)(2,1)S(1)}, f16[128,512]{1,0:T(8,128)(2,1)S(1)}, u32[]{:S(2)}, u32[]{:S(2)}) collective-permute-start(f16[128,512]{1,0:T(8,128)(2,1)S(1)} %collective-permute-done.25), channel_id=1, source_target_pairs={{0,1},{1,0},{2,3},{3,2},{4,5},{5,4},{6,7},{7,6},{8,9},{9,8},{10,11... | collective-permute-start | bytes 393224 | tf_op jit(solution)/shard_map/ppermute | solution.py:393
  113.8 6.3 %collective-permute-start.24 = (f16[128,512]{1,0:T(8,128)(2,1)S(1)}, f16[128,512]{1,0:T(8,128)(2,1)S(1)}, u32[]{:S(2)}, u32[]{:S(2)}) collective-permute-start(f16[128,512]{1,0:T(8,128)(2,1)S(1)} %collective-permute-done.23), channel_id=1, source_target_pairs={{0,1},{1,0},{2,3},{3,2},{4,5},{5,4},{6,7},{7,6},{8,9},{9,8},{10,11... | collective-permute-start | bytes 393224 | tf_op jit(solution)/shard_map/ppermute | solution.py:393
